TPU v7x, 32 devices: a whole 2x2x4 slice. The times are simulated.
32 devices in a mesh: seq: 8 (over z, core), tensor: 4 (over y, x).
Axes of the slice: x: 2, y: 2, z: 4, core: 2. Of those that a mesh axis runs over, the one named last changes fastest.
Arguments:
- tokens: bfloat16 [2560, 5120], P('seq'), may hold values from -6 to 6
- gate_weight: bfloat16 [5120, 13824], P('seq', 'tensor'), may hold values from -0.078125 to 0.078125
- up_weight: bfloat16 [5120, 13824], P('seq', 'tensor'), may hold values from -0.078125 to 0.078125
- cotangent: bfloat16 [2560, 13824], P('seq', 'tensor'), may hold values from -24 to 24
- a_mean: float32 [5120, 128], P('seq'), may hold values from -6 to 6
- a_hess: float32 [5120, 128], P('seq'), may hold values from 0.5 to 8
- a_moment: float32 [5120, 128], P('seq'), may hold values from -3 to 3
- a_noise: float32 [5120, 128], P('seq'), may hold values from -6 to 6
- b_mean: float32 [128, 13824], P('seq', 'tensor'), may hold values from -6 to 6
- b_hess: float32 [128, 13824], P('seq', 'tensor'), may hold values from 0.5 to 8
- b_moment: float32 [128, 13824], P('seq', 'tensor'), may hold values from -3 to 3
- b_noise: float32 [128, 13824], P('seq', 'tensor'), may hold values from -6 to 6
Outputs:
- hidden: bfloat16 [2560, 13824], P('seq', 'tensor')
- grad_tokens: bfloat16 [2560, 5120], P(('seq', 'tensor'))
- a_mean_new: float32 [5120, 128], P('seq')
- a_hess_new: float32 [5120, 128], P('seq')
- a_moment_new: float32 [5120, 128], P('seq')
- b_mean_new: float32 [128, 13824], P('seq', 'tensor')
- b_hess_new: float32 [128, 13824], P('seq', 'tensor')
- b_moment_new: float32 [128, 13824], P('seq', 'tensor')
All inputs are finite; a program needn't handle non-finite values.
Results may differ from a plain program's by a relative error of at most 0.0095.
Values may be sent and summed in bfloat16 or wider, within the bound.
No kernel may reach another device: no remote copies, remote signals or barrier semaphores. Data moves between devices by JAX's collectives and lax.ppermute only.
A program may use at most 256 MiB of HBM per device.

v0:
```python
import math

import jax
import jax.numpy as jnp
from jax import lax
from jax.sharding import PartitionSpec as P

D = 5120
R = 64


ess = 8.0
decay = 0.001
beta_one = 0.9
beta_two = 0.99
rate = 0.1
debias = 1.0 - 0.9**10


def sample(mean, hess, noise):
    scale = jnp.sqrt(ess * (hess + decay))
    return (mean + noise / scale, scale)


def ivon_update(mean, hess, moment, noise, scale, grad):
    hess_hat = grad * noise * scale
    moment_new = beta_one * moment + (1.0 - beta_one) * grad
    diff = hess - hess_hat
    hess_new = (
        beta_two * hess
        + (1.0 - beta_two) * hess_hat
        + 0.5 * (1.0 - beta_two) ** 2 * diff * diff / (hess + decay)
    )
    mean_new = mean - rate * (moment_new / debias + decay * mean) / (hess_new + decay)
    return (mean_new, hess_new, moment_new)


def contract_rows(left, right):
    return lax.dot_general(
        left, right, (((0,), (0,)), ((), ())), preferred_element_type=jnp.float32
    )


def on_device(
    tokens,
    gate_weight,
    up_weight,
    cotangent,
    a_mean,
    a_hess,
    a_moment,
    a_noise,
    b_mean,
    b_hess,
    b_moment,
    b_noise,
):
    a_theta, scale_a = sample(a_mean, a_hess, a_noise)
    b_theta, scale_b = sample(b_mean, b_hess, b_noise)
    a_piece = (a_theta / math.sqrt(D)).astype(jnp.bfloat16)
    b_piece = (b_theta / math.sqrt(R)).astype(jnp.bfloat16)
    a_factor, b_factor = (
        lax.all_gather(a_piece, "seq", axis=0, tiled=True),
        lax.all_gather(b_piece, "seq", axis=0, tiled=True),
    )
    proj = jnp.dot(tokens, a_factor, preferred_element_type=jnp.float32).astype(jnp.bfloat16)
    gate_full, up_full = (
        lax.all_gather(gate_weight, "seq", axis=0, tiled=True),
        lax.all_gather(up_weight, "seq", axis=0, tiled=True),
    )
    gate_base = jnp.dot(tokens, gate_full, preferred_element_type=jnp.float32)
    up_base = jnp.dot(tokens, up_full, preferred_element_type=jnp.float32)
    gate_pre = gate_base + jnp.dot(proj[:, :R], b_factor[:R], preferred_element_type=jnp.float32)
    up_pre = up_base + jnp.dot(proj[:, R:], b_factor[R:], preferred_element_type=jnp.float32)
    sig = jax.nn.sigmoid(gate_pre)
    act = gate_pre * sig
    hidden = (act * up_pre).astype(jnp.bfloat16)
    cot = cotangent.astype(jnp.float32)
    d_gate = (cot * up_pre * sig * (1.0 + gate_pre * (1.0 - sig))).astype(jnp.bfloat16)
    d_up = (cot * act).astype(jnp.bfloat16)
    rank_part = jnp.concatenate(
        [
            jnp.dot(d_gate, b_factor[:R].T, preferred_element_type=jnp.float32),
            jnp.dot(d_up, b_factor[R:].T, preferred_element_type=jnp.float32),
        ],
        axis=1,
    )
    back = jnp.dot(d_gate, gate_full.T, preferred_element_type=jnp.float32)
    back = back + jnp.dot(d_up, up_full.T, preferred_element_type=jnp.float32)
    term = back + jnp.dot(
        rank_part.astype(jnp.bfloat16), a_factor.T, preferred_element_type=jnp.float32
    )
    grad_tokens = lax.psum_scatter(
        term.astype(jnp.bfloat16), "tensor", scatter_dimension=0, tiled=True
    )
    seq_count = lax.axis_size("seq")
    tokens_all = tokens.shape[0] * seq_count
    b_part = jnp.concatenate(
        [contract_rows(proj[:, :R], d_gate), contract_rows(proj[:, R:], d_up)], axis=0
    ) / math.sqrt(tokens_all * R)
    rank_high = rank_part.astype(jnp.bfloat16)
    rank_low = (rank_part - rank_high.astype(jnp.float32)).astype(jnp.bfloat16)
    a_part = (contract_rows(tokens, rank_high) + contract_rows(tokens, rank_low)) / math.sqrt(
        tokens_all * D
    )
    a_seq, b_grad = (
        lax.psum_scatter(
            a_part.astype(jnp.bfloat16), "seq", scatter_dimension=0, tiled=True
        ).astype(jnp.float32),
        lax.psum_scatter(
            b_part.astype(jnp.bfloat16), "seq", scatter_dimension=0, tiled=True
        ).astype(jnp.float32),
    )
    a_grad = lax.psum(a_seq.astype(jnp.bfloat16), "tensor").astype(jnp.float32)
    a_mean_new, a_hess_new, a_moment_new = ivon_update(
        a_mean, a_hess, a_moment, a_noise, scale_a, a_grad
    )
    b_mean_new, b_hess_new, b_moment_new = ivon_update(
        b_mean, b_hess, b_moment, b_noise, scale_b, b_grad
    )
    return (
        hidden,
        grad_tokens,
        a_mean_new,
        a_hess_new,
        a_moment_new,
        b_mean_new,
        b_hess_new,
        b_moment_new,
    )


def solution(mesh):
    in_specs = (
        P("seq", None),
        P("seq", "tensor"),
        P("seq", "tensor"),
        P("seq", "tensor"),
        P("seq", None),
        P("seq", None),
        P("seq", None),
        P("seq", None),
        P("seq", "tensor"),
        P("seq", "tensor"),
        P("seq", "tensor"),
        P("seq", "tensor"),
    )
    out_specs = (
        P("seq", "tensor"),
        P(("seq", "tensor"), None),
        P("seq", None),
        P("seq", None),
        P("seq", None),
        P("seq", "tensor"),
        P("seq", "tensor"),
        P("seq", "tensor"),
    )
    return jax.shard_map(
        on_device, mesh=mesh, in_specs=in_specs, out_specs=out_specs, check_vma=False
    )
```

profile of v0, /device:TPU:0, one launch (start us, length us, event | category | flops | bytes accessed | tf_op | source)
XLA Modules:
  0.0 854.2 jit_solution(12846691120626544954)
XLA Ops:
  7.2 2.0 copy.32
  9.2 1.9 copy.33
  11.1 1.9 copy.34
  13.0 2.0 multiply_convert_fusion.1
  16.7 1.1 multiply_convert_fusion.2
  17.8 22.4 %all_gather.14 = bf16[128,3456]{1,0:T(8,128)(2,1)} all-gather(bf16[16,3456]{1,0:T(8,128)(2,1)S(1)} %multiply_convert_fusion.2), channel_id=1, replica_groups=mesh['seq'=8,'tensor'=4] {'seq'}, dimensions={0}, use_global_device_ids=true | all-gather | bytes 995328 | tf_op jit(solution)/shard_map/all_gather | solution.py:64
  40.2 5.0 all-gather.6.cloned.1.call-done
  45.2 2.3 fusion.10
  47.6 304.0 %all-gather.4.cloned.1.call-done = bf16[5120,3456]{1,0:T(8,128)(2,1)} async-done(((bf16[640,3456]{1,0:T(8,128)(2,1)}), bf16[5120,3456]{1,0:T(8,128)(2,1)}) %all-gather.4.cloned.1.call-update) | async-done | bytes 35389456 | tf_op jit(solution)/shard_map/all_gather | solution.py:68
  351.6 21.0 %fusion.43 = f32[320,3456]{1,0:T(8,128)} fusion(bf16[320,5120]{1,0:T(8,128)(2,1)S(1)} %copy-done, bf16[5120,3456]{1,0:T(8,128)(2,1)} %all-gather.4.cloned.1.call-done), kind=kOutput, calls=%fused_computation.61 | convolution fusion | flops 11324620800 | bytes 43089920 | tf_op jit(solution)/shard_map/dot_general | solution.py:71
  372.6 5.1 convolution_add_fusion.4
  377.6 279.9 %all-gather.8.cloned.1.call-done = bf16[5120,3456]{1,0:T(8,128)(2,1)} async-done(((bf16[640,3456]{1,0:T(8,128)(2,1)}), bf16[5120,3456]{1,0:T(8,128)(2,1)}) %all-gather.8.cloned.1.call-update) | async-done | bytes 35389456 | tf_op jit(solution)/shard_map/all_gather | solution.py:69
  657.5 18.9 %fusion.44 = f32[320,3456]{1,0:T(8,128)} fusion(bf16[320,5120]{1,0:T(8,128)(2,1)S(1)} %copy-done, bf16[5120,3456]{1,0:T(8,128)(2,1)} %all-gather.8.cloned.1.call-done), kind=kOutput, calls=%fused_computation.62 | convolution fusion | flops 11324620800 | bytes 43089920 | tf_op jit(solution)/shard_map/dot_general | solution.py:72
  676.4 6.3 fusion.6
  684.6 0.8 fusion.33
  685.5 2.0 fusion.3
  687.5 2.6 copy.44
  691.0 1.0 copy-done.5
  692.6 1.1 fusion.9
  693.8 20.1 %fusion.45 = f32[320,5120]{1,0:T(8,128)} fusion(bf16[320,3456]{1,0:T(8,128)(2,1)} %copy-done.4, bf16[5120,3456]{1,0:T(8,128)(2,1)} %all-gather.4.cloned.1.call-done), kind=kOutput, calls=%fused_computation.63 | convolution fusion | flops 11324620800 | bytes 44154880 | tf_op jit(solution)/shard_map/dot_general | solution.py:88
  713.9 23.7 %convolution_add_fusion.1 = f32[320,5120]{1,0:T(8,128)} fusion(f32[320,5120]{1,0:T(8,128)} %fusion.45, bf16[320,3456]{1,0:T(8,128)(2,1)S(1)} %copy-done.3, bf16[5120,3456]{1,0:T(8,128)(2,1)} %all-gather.8.cloned.1.call-done), kind=kOutput, calls=%fused_computation.1 | convolution fusion | flops 11326259200 | bytes 50708480 | tf_op jit(solution)/shard_map/dot_general | solution.py:89
  737.6 1.7 copy.45
  739.4 6.0 fusion
  745.5 2.0 copy.35
  747.5 7.8 reduce-scatter.8.cloned.1.call-done
  755.3 2.2 divide_subtract_fusion.1
  757.5 41.3 %all-reduce.2.cloned.1.call-done = bf16[640,128]{0,1:T(8,128)(2,1)} async-done(((bf16[640,128]{0,1:T(8,128)(2,1)}), bf16[640,128]{0,1:T(8,128)(2,1)}) %all-reduce.2.cloned.1.call-update) | async-done | bytes 163856 | tf_op jit(solution)/shard_map/psum | solution.py:114
  798.8 2.5 divide_subtract_fusion
  801.3 1.9 copy.41
  803.2 1.9 copy.42
  805.0 1.9 copy.43
  806.9 40.5 %reduce-scatter.6.cloned.1.call-done = bf16[80,5120]{1,0:T(8,128)(2,1)} async-done(((bf16[320,5120]{1,0:T(8,128)(2,1)}), bf16[80,5120]{1,0:T(8,128)(2,1)}) %reduce-scatter.6.cloned.1.call-update) | async-done | bytes 819216 | tf_op jit(solution)/shard_map/reduce_scatter | solution.py:93
  (40 shorter events, 5.3 us)
Async XLA Ops:
  7.2 38.1 %copy-start = (bf16[320,5120]{1,0:T(8,128)(2,1)S(1)}, bf16[320,5120]{1,0:T(8,128)(2,1)}, u32[]{:S(2)}) copy-start(bf16[320,5120]{1,0:T(8,128)(2,1)} %param.12) | copy-start | bytes 9830404
  7.2 38.1 %all-gather.6.cloned.1.call-start = ((), (), s32[]{:S(2)}) async-start(), calls=%async_computation.4 | async-start | bytes 1474560 | tf_op jit(solution)/shard_map/all_gather | solution.py:63
  15.0 336.6 %all-gather.4.cloned.1.call-start = ((), (), s32[]{:S(2)}) async-start(), calls=%async_computation.3 | async-start | bytes 39813120 | tf_op jit(solution)/shard_map/all_gather | solution.py:68
  15.7 0.9 copy-start.8
  15.8 641.7 %all-gather.8.cloned.1.call-start = ((), (), s32[]{:S(2)}) async-start(), calls=%async_computation.5 | async-start | bytes 39813120 | tf_op jit(solution)/shard_map/all_gather | solution.py:69
  16.5 721.1 %reduce-scatter.10.cloned.1.call-start = ((), (), s32[]{:S(2)}) async-start(), calls=%async_computation.9 | async-start | bytes 1474560
  351.6 21.0 %copy-start.6 = (bf16[128,3456]{1,0:T(8,128)(2,1)S(1)}, bf16[128,3456]{1,0:T(8,128)(2,1)}, u32[]{:S(2)}) copy-start(bf16[128,3456]{1,0:T(8,128)(2,1)} %all_gather.14) | copy-start | bytes 2654212
  657.5 18.9 %copy-start.7 = (bf16[128,3456]{1,0:T(8,128)(2,1)S(1)}, bf16[128,3456]{1,0:T(8,128)(2,1)}, u32[]{:S(2)}) copy-start(bf16[128,3456]{1,0:T(8,128)(2,1)} %all_gather.14) | copy-start | bytes 2654212
  657.5 18.9 %copy-start.10 = (bf16[320,3456]{1,0:T(8,128)(2,1)S(1)}, bf16[320,3456]{1,0:T(8,128)(2,1)}, u32[]{:S(2)}) copy-start(bf16[320,3456]{1,0:T(8,128)(2,1)} %param.15) | copy-start | bytes 6635524
  682.6 1.5 copy-start.2
  682.6 2.0 copy-start.4
  687.5 2.9 copy-start.3
  690.1 65.1 %reduce-scatter.8.cloned.1.call-start = ((), (), s32[]{:S(2)}) async-start(), calls=%async_computation.8 | async-start | bytes 995328 | tf_op jit(solution)/shard_map/reduce_scatter | solution.py:110
  690.4 1.6 copy-start.5
  693.7 105.0 %all-reduce.2.cloned.1.call-start = ((), (), s32[]{:S(2)}) async-start(), calls=%async_computation.7 | async-start | bytes 327680 | tf_op jit(solution)/shard_map/psum | solution.py:114
  739.3 108.0 %reduce-scatter.6.cloned.1.call-start = ((), (), s32[]{:S(2)}) async-start(), calls=%async_computation.6 | async-start | bytes 4096000 | tf_op jit(solution)/shard_map/reduce_scatter | solution.py:93
  745.4 9.8 %copy-start.9 = (f32[16,3456]{1,0:T(8,128)S(1)}, f32[16,3456]{1,0:T(8,128)}, u32[]{:S(2)}) copy-start(f32[16,3456]{1,0:T(8,128)} %param.20) | copy-start | bytes 663556
  745.5 101.9 %copy-start.1 = (bf16[320,5120]{1,0:T(8,128)(2,1)S(1)}, bf16[320,5120]{1,0:T(8,128)(2,1)}, u32[]{:S(2)}) copy-start(bf16[320,5120]{1,0:T(8,128)(2,1)} %param.12) | copy-start | bytes 9830404
Sparse Core Ops, SparseCore 0:
  15.1 30.0 all-gather.5
  46.9 304.6 all-gather.3
  353.2 304.1 all-gather.7
  690.3 32.2 reduce-scatter.9
  724.7 30.5 reduce-scatter.7
  758.0 40.6 all-reduce.1
  802.3 44.9 reduce-scatter.5
where the time goes:
time: 855 us; the launch traced here: 854 us
  waiting for transfers between devices  680 us (80%)
  matrix products  109 us (13%)
  blocking collectives  22.4 us (3%)
  local copies, waits for them, and re-layouts  19.3 us (2%)
  between operations  14.2 us (2%)
  other arithmetic  9.02 us (1%)
    all_gather x1, waiting for transfers between devices, on_device(): lax.all_gather(gate_weight, 'seq', axis=0, tiled=True)  304 us
    all_gather x1, waiting for transfers between devices, on_device(): lax.all_gather(up_weight, 'seq', axis=0, tiled=True)  280 us
    psum x1, waiting for transfers between devices, on_device(): a_grad = lax.psum(a_seq.astype(jnp.bfloat16), 'tensor').astype(jnp.float32)  41.3 us
    reduce_scatter x1, waiting for transfers between devices, on_device(): lax.psum_scatter(term.astype(jnp.bfloat16), 'tensor', scatter_dimension=0...  40.5 us
    dot_general x1, matrix products, on_device(): back = back + jnp.dot(d_up, up_full.T, preferred_element_type=jnp.float32)  23.7 us
    all_gather x1, blocking collectives, on_device(): lax.all_gather(b_piece, 'seq', axis=0, tiled=True)  22.4 us
    dot_general x1, matrix products, on_device(): gate_base = jnp.dot(tokens, gate_full, preferred_element_type=jnp.float32)  21 us
    dot_general x1, matrix products, on_device(): back = jnp.dot(d_gate, gate_full.T, preferred_element_type=jnp.float32)  20.1 us
  transfers between devices with their start and end apart: 7, of which 6 were waited for; matrix products, arithmetic and copies ran while one was open for 11% of the time, Pallas kernels for 0%

commit v1 on v0

v1 whole, which is shorter than its diff:
```python
import functools
import math

import jax
import jax.numpy as jnp
from jax import lax
from jax.experimental import pallas as pl
from jax.experimental.pallas import tpu as pltpu
from jax.sharding import PartitionSpec as P


R = 64
LANE = 128


ess = 8.0
decay = 0.001
beta_one = 0.9
beta_two = 0.99
rate = 0.1
debias = 1.0 - 0.9**10


def sample(mean, hess, noise):
    scale = jnp.sqrt(ess * (hess + decay))
    return (mean + noise / scale, scale)


def ivon_update(mean, hess, moment, noise, scale, grad):
    hess_hat = grad * noise * scale
    moment_new = beta_one * moment + (1.0 - beta_one) * grad
    diff = hess - hess_hat
    hess_new = (
        beta_two * hess
        + (1.0 - beta_two) * hess_hat
        + 0.5 * (1.0 - beta_two) ** 2 * diff * diff / (hess + decay)
    )
    mean_new = mean - rate * (moment_new / debias + decay * mean) / (hess_new + decay)
    return (mean_new, hess_new, moment_new)


def contract_rows(left, right):
    return lax.dot_general(
        left, right, (((0,), (0,)), ((), ())), preferred_element_type=jnp.float32
    )


def contract_lanes(left, right):
    return lax.dot_general(
        left, right, (((1,), (1,)), ((), ())), preferred_element_type=jnp.float32
    )


def gathered_plan(
    tokens,
    gate_weight,
    up_weight,
    cotangent,
    a_mean,
    a_hess,
    a_moment,
    a_noise,
    b_mean,
    b_hess,
    b_moment,
    b_noise,
):
    seq_count = lax.axis_size("seq")
    d_model = gate_weight.shape[0] * seq_count
    tokens_all = tokens.shape[0] * seq_count
    a_theta, scale_a = sample(a_mean, a_hess, a_noise)
    b_theta, scale_b = sample(b_mean, b_hess, b_noise)
    a_piece = (a_theta / math.sqrt(d_model)).astype(jnp.bfloat16)
    b_piece = (b_theta / math.sqrt(R)).astype(jnp.bfloat16)
    a_factor = lax.all_gather(a_piece, "seq", axis=0, tiled=True)
    b_factor = lax.all_gather(b_piece, "seq", axis=0, tiled=True)
    proj = jnp.dot(tokens, a_factor, preferred_element_type=jnp.float32).astype(jnp.bfloat16)
    gate_full = lax.all_gather(gate_weight, "seq", axis=0, tiled=True)
    up_full = lax.all_gather(up_weight, "seq", axis=0, tiled=True)
    gate_base = jnp.dot(tokens, gate_full, preferred_element_type=jnp.float32)
    up_base = jnp.dot(tokens, up_full, preferred_element_type=jnp.float32)
    gate_pre = gate_base + jnp.dot(proj[:, :R], b_factor[:R], preferred_element_type=jnp.float32)
    up_pre = up_base + jnp.dot(proj[:, R:], b_factor[R:], preferred_element_type=jnp.float32)
    sig = jax.nn.sigmoid(gate_pre)
    act = gate_pre * sig
    hidden = (act * up_pre).astype(jnp.bfloat16)
    cot = cotangent.astype(jnp.float32)
    d_gate = (cot * up_pre * sig * (1.0 + gate_pre * (1.0 - sig))).astype(jnp.bfloat16)
    d_up = (cot * act).astype(jnp.bfloat16)
    rank_part = jnp.concatenate(
        [
            jnp.dot(d_gate, b_factor[:R].T, preferred_element_type=jnp.float32),
            jnp.dot(d_up, b_factor[R:].T, preferred_element_type=jnp.float32),
        ],
        axis=1,
    )
    back = jnp.dot(d_gate, gate_full.T, preferred_element_type=jnp.float32)
    back = back + jnp.dot(d_up, up_full.T, preferred_element_type=jnp.float32)
    term = back + jnp.dot(
        rank_part.astype(jnp.bfloat16), a_factor.T, preferred_element_type=jnp.float32
    )
    grad_tokens = lax.psum_scatter(
        term.astype(jnp.bfloat16), "tensor", scatter_dimension=0, tiled=True
    )
    b_part = jnp.concatenate(
        [contract_rows(proj[:, :R], d_gate), contract_rows(proj[:, R:], d_up)], axis=0
    ) / math.sqrt(tokens_all * R)
    rank_high = rank_part.astype(jnp.bfloat16)
    rank_low = (rank_part - rank_high.astype(jnp.float32)).astype(jnp.bfloat16)
    a_part = (contract_rows(tokens, rank_high) + contract_rows(tokens, rank_low)) / math.sqrt(
        tokens_all * d_model
    )
    a_seq = lax.psum_scatter(
        a_part.astype(jnp.bfloat16), "seq", scatter_dimension=0, tiled=True
    ).astype(jnp.float32)
    b_grad = lax.psum_scatter(
        b_part.astype(jnp.bfloat16), "seq", scatter_dimension=0, tiled=True
    ).astype(jnp.float32)
    a_grad = lax.psum(a_seq.astype(jnp.bfloat16), "tensor").astype(jnp.float32)
    a_new = ivon_update(a_mean, a_hess, a_moment, a_noise, scale_a, a_grad)
    b_new = ivon_update(b_mean, b_hess, b_moment, b_noise, scale_b, b_grad)
    return (hidden, grad_tokens, *a_new, *b_new)


def split_rank(value):
    row = lax.broadcasted_iota(jnp.int32, value.shape, 0)
    zero = jnp.zeros_like(value)
    return jnp.concatenate(
        [jnp.where(row < R, value, zero), jnp.where(row >= R, value, zero)], axis=1
    )


def fwd_kernel(zs, cnt, chunk, s_ref, tok_ref, a_ref, b_ref, *refs):
    cot_refs, refs = refs[:zs], refs[zs:]
    w_refs, refs = refs[: 2 * zs], refs[2 * zs :]
    hid_refs, refs = refs[:zs], refs[zs:]
    dg_ref, du_ref, bmat_ref, proj_ref, wcat_s, cot_s, hid_s = refs
    n = pl.program_id(0)
    z, core, col0 = s_ref[0], s_ref[1], s_ref[2]
    tiles = pl.num_programs(0)
    half = a_ref.shape[2]
    part = b_ref.shape[2]
    step = chunk // cnt
    m_all = tok_ref.shape[1] * cnt
    rows = m_all // zs

    def tok(q, m, lanes):
        return tok_ref[q, m // cnt : m // cnt + step, :, lanes].reshape(chunk, -1)

    @pl.when(n == 0)
    def _():
        for m in range(0, m_all, chunk):
            p = jnp.zeros((chunk, 2 * R), jnp.float32)
            for q in range(zs):
                for c in range(2):
                    p += jnp.dot(
                        tok(q, m, slice(c * half, (c + 1) * half)),
                        a_ref[jnp.bitwise_xor(core, c), jnp.bitwise_xor(z, q)],
                        preferred_element_type=jnp.float32,
                    )
            proj_ref[m : m + chunk, :] = p.astype(jnp.bfloat16)

    for k in range(zs):
        q = jnp.bitwise_xor(z, k)
        for side in range(2):
            c = jnp.bitwise_xor(core, side)
            at = pl.ds(pl.multiple_of(c * half, LANE), half)
            w = w_refs[side * zs + k]
            wcat_s[q, at, :LANE] = w[0]
            wcat_s[q, at, LANE:] = w[1]
            at = pl.ds(pl.multiple_of((2 * q + c) * part, part), part)
            bmat_ref[at, :] = b_ref[side, k]
        cot_s[pl.ds(pl.multiple_of(q * rows, 16), rows), :] = cot_refs[k][...]
    keep = col0 + n >= z * tiles
    bb = split_rank(bmat_ref[...])
    for m in range(0, m_all, chunk):
        at = slice(m, m + chunk)
        acc = jnp.dot(proj_ref[at, :], bb, preferred_element_type=jnp.float32)
        for q in range(zs):
            acc += jnp.dot(tok(q, m, slice(None)), wcat_s[q], preferred_element_type=jnp.float32)
        g, u = acc[:, :LANE], acc[:, LANE:]
        sig = jax.nn.sigmoid(g)
        act = g * sig
        hid_s[at, :] = (act * u).astype(jnp.bfloat16)
        cot = cot_s[at, :].astype(jnp.float32)
        dg = cot * u * sig * (1.0 + g * (1.0 - sig))
        dg_ref[at, :] = jnp.where(keep, dg, 0.0).astype(jnp.bfloat16)
        du_ref[at, :] = jnp.where(keep, cot * act, 0.0).astype(jnp.bfloat16)
    for k in range(zs):
        q = jnp.bitwise_xor(z, k)
        hid_refs[k][...] = hid_s[pl.ds(pl.multiple_of(q * rows, 16), rows), :]


def bwd_kernel(zs, ts, cnt, s_ref, dg_ref, du_ref, bmat_ref, a_ref, *refs):
    w_refs, (out_ref, rank_ref, d_s) = refs[: 2 * zs], refs[2 * zs :]
    i = pl.program_id(0)
    z, core = s_ref[0], s_ref[1]
    wide = dg_ref.shape[1]

    @pl.when(i == 0)
    def _():
        d_s[:, :wide] = dg_ref[...]
        d_s[:, wide : 2 * wide] = du_ref[...]
        rank = contract_lanes(d_s[:, : 2 * wide], split_rank(bmat_ref[...]))
        rank_ref[...] = rank
        d_s[:, 2 * wide :] = rank.astype(jnp.bfloat16)

    for k in range(zs):
        q = jnp.bitwise_xor(z, k)
        w = []
        for side in range(2):
            ref = w_refs[side * zs + k]
            w.append(jnp.concatenate([ref[0], ref[1], a_ref[side, k]], axis=1))
        w = jnp.concatenate(w, axis=0)
        acc = contract_lanes(d_s[...], w).astype(jnp.bfloat16)
        for side in range(2):
            blk = 2 * q + jnp.bitwise_xor(core, side)
            part = acc[:, side * LANE : (side + 1) * LANE]
            for zz in range(zs):
                for t in range(ts):
                    m = (zz * ts + t) * cnt
                    out_ref[t, zz, blk] = part[m : m + cnt, :]


def place_kernel(zs, ts, own, sizes, wide, limit, s_ref, *refs):
    out_ref = refs[-1]
    for k in range(zs):
        at = jnp.minimum(jnp.bitwise_xor(s_ref[0], k) * wide, limit)
        at = pl.ds(pl.multiple_of(at, LANE), wide)
        for j, (off, cnt) in enumerate(sizes):
            for t in range(ts):
                out_ref[t * own + off : t * own + off + cnt, at] = refs[j * zs + k][
                    t * cnt : (t + 1) * cnt, :
                ]


def whole(shape):
    return pl.BlockSpec(shape, lambda i, s: (0,) * len(shape), pipeline_mode=pl.Buffered(1))


def forward(scalars, tok, a_all, b_all, cots, weights, off, cnt):
    zs, groups, _, quarter = tok.shape
    m_all = groups * cnt
    rows, wide = cots[0].shape
    half = weights[0].shape[1]
    chunk = m_all // max(1, m_all // 256)
    while chunk % cnt or m_all % chunk:
        chunk += 16
    bf = jnp.bfloat16
    return pl.pallas_call(
        functools.partial(fwd_kernel, zs, cnt, chunk),
        grid_spec=pltpu.PrefetchScalarGridSpec(
            num_scalar_prefetch=1,
            grid=(wide // LANE,),
            in_specs=[
                pl.BlockSpec(
                    (zs, groups, cnt, quarter),
                    lambda i, s: (0, 0, off // cnt, 0),
                    pipeline_mode=pl.Buffered(1),
                ),
                whole(a_all.shape),
                pl.BlockSpec((*b_all.shape[:3], LANE), lambda i, s: (0, 0, 0, i)),
            ]
            + [pl.BlockSpec((rows, LANE), lambda i, s: (0, i))] * zs
            + [pl.BlockSpec((2, half, LANE), lambda i, s: (0, 0, i))] * (2 * zs),
            out_specs=[pl.BlockSpec((rows, LANE), lambda i, s: (0, i))] * zs
            + [pl.BlockSpec((m_all, LANE), lambda i, s: (0, i))] * 2
            + [pl.BlockSpec((2 * R, LANE), lambda i, s: (0, i))]
            + [pl.BlockSpec((m_all, 2 * R), lambda i, s: (0, 0))],
            scratch_shapes=[
                pltpu.VMEM((zs, 2 * half, 2 * LANE), bf),
                pltpu.VMEM((m_all, LANE), bf),
                pltpu.VMEM((m_all, LANE), bf),
            ],
        ),
        out_shape=[jax.ShapeDtypeStruct((rows, wide), bf)] * zs
        + [jax.ShapeDtypeStruct((m_all, wide), bf)] * 2
        + [jax.ShapeDtypeStruct((2 * R, wide), bf)]
        + [jax.ShapeDtypeStruct((m_all, 2 * R), bf)],
        compiler_params=pltpu.CompilerParams(vmem_limit_bytes=44 << 20),
        cost_estimate=pl.CostEstimate(
            flops=2 * m_all * 2 * wide * (2 * zs * half),
            bytes_accessed=4 * zs * half * wide * 2 + m_all * (zs * quarter + 4 * wide) * 2,
            transcendentals=m_all * wide,
        ),
        name="fwd_columns",
    )(scalars, tok, a_all, b_all, *cots, *weights)


def backward(scalars, d_gate, d_up, bmat, a_all, weights, ts, cnt):
    zs = len(weights) // 2
    m_all, wide = d_gate.shape
    half = weights[0].shape[1]
    bf = jnp.bfloat16
    return pl.pallas_call(
        functools.partial(bwd_kernel, zs, ts, cnt),
        grid_spec=pltpu.PrefetchScalarGridSpec(
            num_scalar_prefetch=1,
            grid=(half // LANE,),
            in_specs=[whole(d_gate.shape), whole(d_up.shape), whole(bmat.shape)]
            + [pl.BlockSpec((2, zs, LANE, 2 * R), lambda i, s: (0, 0, i, 0))]
            + [pl.BlockSpec((2, LANE, wide), lambda i, s: (0, i, 0))] * (2 * zs),
            out_specs=[
                pl.BlockSpec((ts, zs, 2 * zs, cnt, LANE), lambda i, s: (0, 0, 0, 0, i)),
                pl.BlockSpec((m_all, 2 * R), lambda i, s: (0, 0)),
            ],
            scratch_shapes=[pltpu.VMEM((m_all, 2 * wide + 2 * R), bf)],
        ),
        out_shape=[
            jax.ShapeDtypeStruct((ts, zs, 2 * zs, cnt, half), bf),
            jax.ShapeDtypeStruct((m_all, 2 * R), jnp.float32),
        ],
        compiler_params=pltpu.CompilerParams(vmem_limit_bytes=44 << 20),
        cost_estimate=pl.CostEstimate(
            flops=2 * m_all * 2 * wide * (2 * zs * half),
            bytes_accessed=4 * zs * half * wide * 2 + m_all * (2 * zs * half + 2 * wide) * 2,
            transcendentals=0,
        ),
        name="bwd_columns",
    )(scalars, d_gate, d_up, bmat, a_all, *weights)


def place(scalars, pieces, zs, ts, own, sizes, cols):
    wide = pieces[0].shape[1]
    return pl.pallas_call(
        functools.partial(place_kernel, zs, ts, own, sizes, wide, cols - wide),
        grid_spec=pltpu.PrefetchScalarGridSpec(
            num_scalar_prefetch=1,
            grid=(1,),
            in_specs=[whole(piece.shape) for piece in pieces],
            out_specs=whole((ts * own, cols)),
        ),
        out_shape=jax.ShapeDtypeStruct((ts * own, cols), jnp.bfloat16),
        compiler_params=pltpu.CompilerParams(vmem_limit_bytes=16 << 20),
        cost_estimate=pl.CostEstimate(
            flops=0, bytes_accessed=4 * ts * own * cols, transcendentals=0
        ),
        name="place_hidden",
    )(scalars, *pieces)


def after(value, *earlier):
    return lax.optimization_barrier((value, *earlier))[0]


def chunk_sizes(own):
    sizes, off = [], 0
    size = max(16, own * 2 // 5 // 16 * 16)
    while off < own:
        cnt = min(size, own - off)
        while off % cnt:
            cnt -= 16
        sizes.append((off, cnt))
        off += cnt
    return tuple(sizes)


def split_plan(
    tokens,
    gate_weight,
    up_weight,
    cotangent,
    a_mean,
    a_hess,
    a_moment,
    a_noise,
    b_mean,
    b_hess,
    b_moment,
    b_noise,
):
    seq_count = lax.axis_size("seq")
    ts = lax.axis_size("tensor")
    zs = seq_count // 2
    half, cols = gate_weight.shape
    d_model = half * seq_count
    rows = tokens.shape[0]
    tokens_all = rows * seq_count
    wide = -(-cols // (zs * LANE)) * LANE
    own = rows // ts
    part = 2 * R // seq_count
    seq = lax.axis_index("seq")
    z, core = seq // 2, seq % 2
    tensor = lax.axis_index("tensor")
    cores = [[2 * j + c for j in range(zs)] for c in range(2)]
    bf = jnp.bfloat16

    def start_of(chip):
        return jnp.minimum(chip * wide, cols - wide)

    def columns(value, k):
        at = start_of(jnp.bitwise_xor(z, k))
        return lax.dynamic_slice_in_dim(value, at, wide, value.ndim - 1)

    def over_z(value, k):
        if k == 0:
            return value
        return lax.ppermute(value, "seq", [(s, s ^ (2 * k)) for s in range(seq_count)])

    def over_core(value):
        return lax.ppermute(value, "seq", [(s, s ^ 1) for s in range(seq_count)])

    scalars = jnp.stack([z, core, start_of(z) // LANE]).astype(jnp.int32)

    a_theta, scale_a = sample(a_mean, a_hess, a_noise)
    b_theta, scale_b = sample(b_mean, b_hess, b_noise)
    a_piece = (a_theta / math.sqrt(d_model)).astype(bf)
    b_piece = (b_theta / math.sqrt(R)).astype(bf)
    a_mine = jnp.stack([over_z(a_piece, k) for k in range(zs)])
    b_mine = jnp.stack([over_z(columns(b_piece, k), k) for k in range(zs)])
    a_all = jnp.stack([a_mine, over_core(a_mine)])
    b_all = jnp.stack([b_mine, over_core(b_mine)])

    pieces = [jnp.stack([columns(gate_weight, k), columns(up_weight, k)]) for k in range(zs)]
    mine = [None] * zs
    mine[0] = pieces[0]
    for k in range(zs - 1, 0, -1):
        mine[k] = over_z(pieces[k], k)
    weights = mine + [over_core(piece) for piece in mine]

    quarter = d_model // ts
    tok = lax.dynamic_slice_in_dim(tokens, tensor * quarter, quarter, 1)
    tok = after(tok, *pieces)
    tok = lax.all_gather(tok, "seq", axis=0, axis_index_groups=cores, tiled=True)
    tok = lax.all_gather(tok, "tensor", axis=0, tiled=False)

    sizes = chunk_sizes(own)
    cots, gate = [], mine[zs - 1]
    for off, cnt in sizes:
        cot = cotangent.reshape(ts, own, cols)[:, off : off + cnt].reshape(ts * cnt, cols)
        cots.append(
            [over_z(after(columns(cot, k), gate) if k else columns(cot, k), k) for k in range(zs)]
        )
        gate = mine[zs - 1], mine[zs - 2]
    tok = tok.reshape(zs, zs * ts, own, quarter)

    hidden, grads, ranks = [], [], []
    b_part = jnp.zeros((2 * R, wide), jnp.float32)
    for (off, cnt), cot in zip(sizes, cots):
        *hid, d_gate, d_up, bmat, proj = forward(scalars, tok, a_all, b_all, cot, weights, off, cnt)
        hidden += [over_z(hid[k], k) for k in range(zs)]
        term, rank = backward(scalars, d_gate, d_up, bmat, a_all, weights, ts, cnt)
        ranks.append(rank.reshape(zs * ts, cnt, 2 * R))
        b_part = b_part + jnp.concatenate(
            [contract_rows(proj[:, :R], d_gate), contract_rows(proj[:, R:], d_up)], axis=0
        )
        term = lax.psum_scatter(
            term.reshape(-1, half), "tensor", scatter_dimension=0, tiled=True
        ).reshape(term.shape[1:])
        total = jnp.zeros(term.shape[1:], jnp.float32)
        for k in range(zs):
            piece = lax.dynamic_index_in_dim(term, jnp.bitwise_xor(z, k), 0, keepdims=False)
            total = total + over_z(piece, k).astype(jnp.float32)
        grads.append(total.astype(bf))

    hidden = place(scalars, hidden, zs, ts, own, sizes, cols)
    grad_tokens = jnp.concatenate(grads, axis=1).transpose(1, 0, 2).reshape(own, d_model)

    rank = jnp.concatenate(ranks, axis=1).reshape(zs * rows, 2 * R)
    rank_high = rank.astype(bf)
    rank_low = (rank - rank_high.astype(jnp.float32)).astype(bf)
    both = jnp.concatenate([rank_high, rank_low], axis=1)
    a_part = jnp.einsum(
        "qmd,mr->qdr",
        tok.reshape(zs, zs * rows, quarter),
        both,
        preferred_element_type=jnp.float32,
    )
    a_part = (a_part[..., : 2 * R] + a_part[..., 2 * R :]) / math.sqrt(tokens_all * d_model)
    a_part = a_part.reshape(zs, 2, half, 2 * R)
    a_keep = lax.dynamic_index_in_dim(a_part, core, 1, keepdims=False)
    a_give = lax.dynamic_index_in_dim(a_part, 1 - core, 1, keepdims=False)
    a_part = (a_keep + over_core(a_give.astype(bf)).astype(jnp.float32)).astype(bf)
    a_seq = jnp.zeros((half, 2 * R), jnp.float32)
    for k in range(zs):
        piece = lax.dynamic_index_in_dim(a_part, jnp.bitwise_xor(z, k), 0, keepdims=False)
        a_seq = a_seq + over_z(piece, k).astype(jnp.float32)
    a_seq = a_seq.astype(bf)
    a_grad = a_seq.astype(jnp.float32)
    for k in range(1, ts):
        a_grad = a_grad + lax.ppermute(
            a_seq, "tensor", [(t, t ^ k) for t in range(ts)]
        ).astype(jnp.float32)

    b_part = (b_part / math.sqrt(tokens_all * R)).astype(bf)
    b_parts = lax.all_to_all(
        b_part.reshape(seq_count, part, wide), "seq", 0, 0, tiled=True
    ).astype(jnp.float32)
    b_parts = b_parts.reshape(zs, 2, part, wide).sum(1)
    b_grad = jnp.concatenate(
        [b_parts[j] for j in range(zs - 1)]
        + [b_parts[zs - 1][:, wide - (cols - (zs - 1) * wide) :]],
        axis=1,
    )

    a_new = ivon_update(a_mean, a_hess, a_moment, a_noise, scale_a, a_grad)
    b_new = ivon_update(b_mean, b_hess, b_moment, b_noise, scale_b, b_grad)
    return (hidden, grad_tokens, *a_new, *b_new)


def on_device(tokens, gate_weight, *rest):
    seq_count, ts = lax.axis_size("seq"), lax.axis_size("tensor")
    zs = seq_count // 2
    half, cols = gate_weight.shape
    rows = tokens.shape[0]
    wide = -(-cols // (zs * LANE)) * LANE
    fits = (
        seq_count == 2 * ts
        and ts & (ts - 1) == 0
        and half % LANE == 0
        and cols % LANE == 0
        and (zs - 1) * wide < cols
        and rows % (16 * ts) == 0
        and 2 * R == 16 * seq_count
        and rows * zs * half * seq_count * 2 <= 16 << 20
    )
    plan = split_plan if fits else gathered_plan
    return plan(tokens, gate_weight, *rest)


def solution(mesh):
    row, both = P("seq", None), P("seq", "tensor")
    in_specs = (row, both, both, both, row, row, row, row, both, both, both, both)
    out_specs = (both, P(("seq", "tensor"), None), row, row, row, both, both, both)
    return jax.shard_map(
        on_device, mesh=mesh, in_specs=in_specs, out_specs=out_specs, check_vma=False
    )
```

time: 855 us -> 684 us (0.80)
  waiting for transfers between devices: 680 us -> 341 us
  starting transfers between devices: 0.46 us -> 145 us
  Pallas kernels: 0 us -> 109 us
  matrix products: 109 us -> 8.92 us
  local copies, waits for them, and re-layouts: 19.3 us -> 43 us
  blocking collectives: 22.4 us -> 0 us
  other arithmetic: 9.02 us -> 21.8 us
    all_gather x3 -> x2, waiting for transfers between devices: 589 us -> 68.4 us  [the longest x1 68.4 us: split_plan(): lax.all_gather(tok, 'seq', axis=0, axis_index_groups=cores, tiled=True)]
    ppermute x0 -> x49, waiting for transfers between devices: none -> 272 us  [the longest x39 272 us: over_z(): lax.ppermute(value, 'seq', [(s, s ^ 2 * k) for s in range(seq_count)])]
    ppermute x0 -> x49, starting transfers between devices: none -> 140 us  [the longest x39 135 us: over_z(): lax.ppermute(value, 'seq', [(s, s ^ 2 * k) for s in range(seq_count)])]
    pallas_call x0 -> x7, Pallas kernels: none -> 109 us  [the longest x3 59.6 us: forward(): pl.pallas_call(functools.partial(fwd_kernel, zs, cnt, chunk), grid_spec=p...]
    dot_general x10 -> x1, matrix products: 105 us -> 7.01 us  [split_plan(): jnp.einsum('qmd,mr->qdr', tok.reshape(zs, zs * rows, quarter), both, pref...]
    reduce_scatter x2 -> x3, waiting for transfers between devices: 48.3 us -> 0.02 us  [split_plan(): lax.psum_scatter(term.reshape(-1, half), 'tensor', scatter_dimension=0, t...]
    psum x1 -> x0, waiting for transfers between devices: 41.3 us -> none  [on_device(): a_grad = lax.psum(a_seq.astype(jnp.bfloat16), 'tensor').astype(jnp.float32)]
    all_gather x1 -> x0, blocking collectives: 22.4 us -> none  [on_device(): lax.all_gather(b_piece, 'seq', axis=0, tiled=True)]
  transfers between devices with their start and end apart: 7 -> 55, of which waited for: 6 -> 24; matrix products, arithmetic and copies ran while one was open for 11% -> 6% of each run, Pallas kernels for 0% -> 12%
where the time goes in v1:
time: 684 us; the launch traced here: 683 us
  waiting for transfers between devices  341 us (50%)
  starting transfers between devices  145 us (21%)
  Pallas kernels  109 us (16%)
  local copies, waits for them, and re-layouts  43 us (6%)
  other arithmetic  21.8 us (3%)
  between operations  14.7 us (2%)
  matrix products  8.92 us (1%)
    ppermute x39, waiting for transfers between devices, over_z(): lax.ppermute(value, 'seq', [(s, s ^ 2 * k) for s in range(seq_count)])  272 us
    ppermute x39, starting transfers between devices, over_z(): lax.ppermute(value, 'seq', [(s, s ^ 2 * k) for s in range(seq_count)])  135 us
    all_gather x1, waiting for transfers between devices, split_plan(): lax.all_gather(tok, 'seq', axis=0, axis_index_groups=cores, tiled=True)  68.4 us
    pallas_call x3, Pallas kernels, forward(): pl.pallas_call(functools.partial(fwd_kernel, zs, cnt, chunk), grid_spec=p...  59.6 us
    pallas_call x3, Pallas kernels, backward(): pl.pallas_call(functools.partial(bwd_kernel, zs, ts, cnt), grid_spec=pltp...  46.1 us
    unnamed x133, local copies, waits for them, and re-layouts  20.3 us
  transfers between devices with their start and end apart: 55, of which 24 were waited for; matrix products, arithmetic and copies ran while one was open for 6% of the time, Pallas kernels for 12%

profile of v1, /device:TPU:0, one launch (start us, length us, event | category | flops | bytes accessed | tf_op | source)
XLA Modules:
  0.0 683.1 jit_solution(15958636330485398843)
XLA Ops:
  10.1 9.4 %dynamic-slice_bitcast_fusion = (bf16[1,640,896]{2,1,0:T(8,128)(2,1)S(1)}, bf16[1,640,896]{2,1,0:T(8,128)(2,1)S(1)}, bf16[1,640,896]{2,1,0:T(8,128)(2,1)S(1)}, b...) fusion(bf16[640,3456]{1,0:T(8,128)(2,1)} %param.14, ...), kind=kLoop, calls=%fused_computation.10 | loop fusion | bytes 18350096 | tf_op jit(solution)/shard_map/stack | solution.py:414
  24.7 68.4 %all-gather.4.cloned.1.call-done = bf16[1280,1280]{1,0:T(8,128)(2,1)} async-done(((bf16[320,1280]{1,0:T(8,128)(2,1)}), bf16[1280,1280]{1,0:T(8,128)(2,1)}) %all-gather.4.cloned.1.call-update) | async-done | bytes 3276816 | tf_op jit(solution)/shard_map/all_gather | solution.py:424
  97.8 95.7 %collective-permute-done.12.refs_5_.refs_1_ = bf16[2,640,896]{2,1,0:T(8,128)(2,1)} collective-permute-done((bf16[2,640,896]{2,1,0:T(8,128)(2,1)}, bf16[2,640,896]{2,1,0:T(8,128)(2,1)}, u32[]{:S(2)}, u32[]{:S(2)}) %collective-permute-start.12) | collective-permute-done | bytes 2293792 | tf_op jit(solution)/shard_map/ppermute | solution.py:398
  193.5 52.3 %collective-permute-done.13.refs_6_.refs_2_ = bf16[2,640,896]{2,1,0:T(8,128)(2,1)} collective-permute-done((bf16[2,640,896]{2,1,0:T(8,128)(2,1)}, bf16[2,640,896]{2,1,0:T(8,128)(2,1)}, u32[]{:S(2)}, u32[]{:S(2)}) %collective-permute-start.13) | collective-permute-done | bytes 2293792 | tf_op jit(solution)/shard_map/ppermute | solution.py:398
  253.4 47.4 %collective-permute-start.5 = (bf16[16,896]{1,0:T(8,128)(2,1)S(1)}, bf16[16,896]{1,0:T(8,128)(2,1)S(1)}, u32[]{:S(2)}, u32[]{:S(2)}) collective-permute-start(bf16[16,896]{1,0:T(8,128)(2,1)S(1)} %get-tuple-element.143), channel_id=1, source_target_pairs={{0,16},{4,20},{8,24},{12,28},{16,0},{20,4},{24,8},{28,12},{1,17},{... | collective-permute-start | bytes 86024 | tf_op jit(solution)/shard_map/ppermute | solution.py:398
  308.8 5.2 collective-permute-done.2
  314.0 6.1 collective-permute-start.1
  320.1 4.1 collective-permute-done.1
  343.5 4.7 collective-permute-done.28.refs_2_
  354.3 15.2 %fwd_columns.5 = (bf16[64,896]{1,0:T(8,128)(2,1)S(1)}, bf16[64,896]{1,0:T(8,128)(2,1)S(1)}, bf16[64,896]{1,0:T(8,128)(2,1)S(1)}, bf16[64,896]{1,0:T(8,128)(2,1)S...) custom-call(s32[3]{0:T(128)S(1)} %copy-done.37, ...), custom_call_target="tpu_custom_call" | custom-call | flops 4697620480 | bytes 22806528 | tf_op jit(solution)/shard_map/fwd_columns/pallas_call | solution.py:250
  372.6 11.9 %bwd_columns.5 = (bf16[4,4,8,16,640]{4,3,2,1,0:T(8,128)(2,1)}, f32[256,128]{1,0:T(8,128)S(1)}) custom-call(s32[3]{0:T(128)S(1)} %copy-done.37, bf16[256,896]{1,0:T(8,128)(2,1)S(1)} %get-tuple-element.78.dg_ref, bf16[256,896]{1,0:T(8,128)(2,1)S(1)} %get-tuple-element.79.du_ref, bf16[128,896]{1,0:T(8,128)(2,1)S(1)} %get-tuple-element.80.bmat_ref, ...), custom_call_target="tpu_custom_call" | custom-call | flops 4697620480 | bytes 21889024 | tf_op jit(solution)/shard_map/bwd_columns/pallas_call | solution.py:295
  393.2 6.0 collective-permute-done.21.refs_1_
  399.2 10.5 %collective-permute-done.22.refs_2_ = bf16[128,896]{1,0:T(8,128)(2,1)S(1)} collective-permute-done((bf16[128,896]{1,0:T(8,128)(2,1)S(1)}, bf16[128,896]{1,0:T(8,128)(2,1)S(1)}, u32[]{:S(2)}, u32[]{:S(2)}) %collective-permute-start.22) | collective-permute-done | bytes 229408 | tf_op jit(solution)/shard_map/ppermute | solution.py:398
  409.7 22.1 %fwd_columns.4 = (bf16[128,896]{1,0:T(8,128)(2,1)S(1)}, bf16[128,896]{1,0:T(8,128)(2,1)S(1)}, bf16[128,896]{1,0:T(8,128)(2,1)S(1)}, bf16[128,896]{1,0:T(8,128)(2...) custom-call(s32[3]{0:T(128)S(1)} %copy-done.38, ...), custom_call_target="tpu_custom_call" | custom-call | flops 9395240960 | bytes 27262976 | tf_op jit(solution)/shard_map/fwd_columns/pallas_call | solution.py:250
  433.1 17.1 %bwd_columns.4 = (bf16[4,4,8,32,640]{4,3,2,1,0:T(8,128)(2,1)}, f32[512,128]{1,0:T(8,128)S(1)}) custom-call(s32[3]{0:T(128)S(1)} %copy-done.38, bf16[512,896]{1,0:T(8,128)(2,1)S(1)} %get-tuple-element.74.dg_ref, bf16[512,896]{1,0:T(8,128)(2,1)S(1)} %get-tuple-element.75.du_ref, bf16[128,896]{1,0:T(8,128)(2,1)S(1)} %get-tuple-element.76.bmat_ref, ...), custom_call_target="tpu_custom_call" | custom-call | flops 9395240960 | bytes 25427968 | tf_op jit(solution)/shard_map/bwd_columns/pallas_call | solution.py:295
  451.3 4.1 collective-permute-start.9
  457.8 4.3 collective-permute-done.9.refs_1_
  462.1 11.5 %collective-permute-done.10.refs_2_ = bf16[128,896]{1,0:T(8,128)(2,1)S(1)} collective-permute-done((bf16[128,896]{1,0:T(8,128)(2,1)}, bf16[128,896]{1,0:T(8,128)(2,1)S(1)}, u32[]{:S(2)}, u32[]{:S(2)}) %collective-permute-start.10) | collective-permute-done | bytes 229408 | tf_op jit(solution)/shard_map/ppermute | solution.py:398
  476.1 22.4 %fwd_columns.3 = (bf16[128,896]{1,0:T(8,128)(2,1)S(1)}, bf16[128,896]{1,0:T(8,128)(2,1)S(1)}, bf16[128,896]{1,0:T(8,128)(2,1)S(1)}, bf16[128,896]{1,0:T(8,128)(2...) custom-call(s32[3]{0:T(128)S(1)} %copy-done.38, ...), custom_call_target="tpu_custom_call" | custom-call | flops 9395240960 | bytes 27262976 | tf_op jit(solution)/shard_map/fwd_columns/pallas_call | solution.py:250
  499.2 17.1 %bwd_columns.3 = (bf16[4,4,8,32,640]{4,3,2,1,0:T(8,128)(2,1)}, f32[512,128]{1,0:T(8,128)S(1)}) custom-call(s32[3]{0:T(128)S(1)} %copy-done.38, bf16[512,896]{1,0:T(8,128)(2,1)S(1)} %get-tuple-element.70.dg_ref, bf16[512,896]{1,0:T(8,128)(2,1)S(1)} %get-tuple-element.71.du_ref, bf16[128,896]{1,0:T(8,128)(2,1)S(1)} %get-tuple-element.72.bmat_ref, ...), custom_call_target="tpu_custom_call" | custom-call | flops 9395240960 | bytes 25427968 | tf_op jit(solution)/shard_map/bwd_columns/pallas_call | solution.py:295
  528.1 7.0 %fusion.3 = f32[4,1280,256]{2,1,0:T(8,128)S(1)} fusion(bf16[4,1280,1280]{2,1,0:T(8,128)(2,1)} %bitcast.148, bf16[1280,128]{1,0:T(8,128)(2,1)S(1)} %get-tuple-element.94, bf16[1280,128]{1,0:T(8,128)(2,1)S(1)} %get-tuple-element.95), kind=kOutput, calls=%fused_computation.23 | convolution fusion | flops 3356753920 | bytes 19005440 | tf_op jit(solution)/shard_map/qmd,mr->qdr/dot_general | solution.py:463
  537.7 3.7 all-to-all-start
  551.8 3.4 collective-permute-done.20.refs_3_
  555.2 4.7 collective-permute-done.24.refs_5_
  559.9 15.3 %collective-permute-done.25.refs_6_ = bf16[128,896]{1,0:T(8,128)(2,1)S(1)} collective-permute-done((bf16[128,896]{1,0:T(8,128)(2,1)S(1)}, bf16[128,896]{1,0:T(8,128)(2,1)S(1)}, u32[]{:S(2)}, u32[]{:S(2)}) %collective-permute-start.25) | collective-permute-done | bytes 229408 | tf_op jit(solution)/shard_map/ppermute | solution.py:398
  581.3 5.6 collective-permute-start.44
  588.0 10.4 %collective-permute-done.44 = bf16[640,128]{1,0:T(8,128)(2,1)S(1)} collective-permute-done((bf16[640,128]{1,0:T(8,128)(2,1)S(1)}, bf16[640,128]{1,0:T(8,128)(2,1)S(1)}, u32[]{:S(2)}, u32[]{:S(2)}) %collective-permute-start.44) | collective-permute-done | bytes 163872 | tf_op jit(solution)/shard_map/ppermute | solution.py:398
  617.9 12.7 %collective-permute-done.40 = bf16[8,16,640]{2,0,1:T(8,128)(2,1)} collective-permute-done((bf16[8,16,640]{2,0,1:T(8,128)(2,1)S(1)}, bf16[8,16,640]{2,0,1:T(8,128)(2,1)}, u32[]{:S(2)}, u32[]{:S(2)}) %collective-permute-start.40) | collective-permute-done | bytes 163872 | tf_op jit(solution)/shard_map/ppermute | solution.py:398
  630.6 4.9 collective-permute-start.35
  635.6 17.6 %collective-permute-start.33 = (bf16[8,32,640]{2,0,1:T(8,128)(2,1)S(1)}, bf16[8,32,640]{2,0,1:T(8,128)(2,1)S(1)}, u32[]{:S(2)}, u32[]{:S(2)}) collective-permute-start(bf16[8,32,640]{2,0,1:T(8,128)(2,1)S(1)} %bitcast.169), channel_id=1, source_target_pairs={{0,8},{4,12},{8,0},{12,4},{16,24},{20,28},{24,16},{28,20},{1,9},{5... | collective-permute-start | bytes 983048 | tf_op jit(solution)/shard_map/ppermute | solution.py:398
  654.3 6.1 collective-permute-done.37
  660.7 13.6 %collective-permute-done.34 = bf16[8,32,640]{2,0,1:T(8,128)(2,1)S(1)} collective-permute-done((bf16[8,32,640]{2,0,1:T(8,128)(2,1)S(1)}, bf16[8,32,640]{2,0,1:T(8,128)(2,1)S(1)}, u32[]{:S(2)}, u32[]{:S(2)}) %collective-permute-start.34) | collective-permute-done | bytes 327712 | tf_op jit(solution)/shard_map/ppermute | solution.py:398
  (277 shorter events, 127.9 us)
Async XLA Ops:
  7.2 85.9 %all-gather.4.cloned.1.call-start = ((), (), s32[]{:S(2)}) async-start(), calls=%async_computation.4 | async-start | bytes 4096000 | tf_op jit(solution)/shard_map/all_gather | solution.py:424
  24.6 324.9 %all-gather.6.cloned.1.call-start = ((), (), s32[]{:S(2)}) async-start(), calls=%async_computation.8 | async-start | bytes 16384000 | tf_op jit(solution)/shard_map/all_gather | solution.py:425
  93.1 508.9 %reduce-scatter.8.cloned.1.call-start = ((), (), s32[]{:S(2)}) async-start(), calls=%async_computation.7 | async-start | bytes 3276800 | tf_op jit(solution)/shard_map/reduce_scatter | solution.py:447
  93.4 100.1 %collective-permute-start.12 = (bf16[2,640,896]{2,1,0:T(8,128)(2,1)}, bf16[2,640,896]{2,1,0:T(8,128)(2,1)}, u32[]{:S(2)}, u32[]{:S(2)}) collective-permute-start(bf16[2,640,896]{2,1,0:T(8,128)(2,1)} %pad_maximum_fusion.1), channel_id=1, source_target_pairs={{0,8},{4,12},{8,0},{12,4},{16,24},{20,28},{24,16},{28,20},{1,9},{5... | collective-permute-start | bytes 6881288 | tf_op jit(solution)/shard_map/ppermute | solution.py:398
  93.4 152.3 %collective-permute-start.13 = (bf16[2,640,896]{2,1,0:T(8,128)(2,1)}, bf16[2,640,896]{2,1,0:T(8,128)(2,1)}, u32[]{:S(2)}, u32[]{:S(2)}) collective-permute-start(bf16[2,640,896]{2,1,0:T(8,128)(2,1)} %pad_maximum_fusion.2), channel_id=1, source_target_pairs={{0,16},{4,20},{8,24},{12,28},{16,0},{20,4},{24,8},{28,12},{1,17},{... | collective-permute-start | bytes 6881288 | tf_op jit(solution)/shard_map/ppermute | solution.py:398
  94.7 151.0 %collective-permute-start.8 = (bf16[2,640,896]{2,1,0:T(8,128)(2,1)}, bf16[2,640,896]{2,1,0:T(8,128)(2,1)}, u32[]{:S(2)}, u32[]{:S(2)}) collective-permute-start(bf16[2,640,896]{2,1,0:T(8,128)(2,1)} %pad_maximum_fusion.3), channel_id=1, source_target_pairs={{0,24},{4,28},{8,16},{12,20},{16,8},{20,12},{24,0},{28,4},{1,25},{... | collective-permute-start | bytes 6881288 | tf_op jit(solution)/shard_map/ppermute | solution.py:398
  97.8 238.7 %collective-permute-start.14 = (bf16[2,640,896]{2,1,0:T(8,128)(2,1)S(1)}, bf16[2,640,896]{2,1,0:T(8,128)(2,1)}, u32[]{:S(2)}, u32[]{:S(2)}) collective-permute-start(bf16[2,640,896]{2,1,0:T(8,128)(2,1)S(1)} %pad_maximum_fusion.refs_4_.refs_0_), channel_id=1, source_target_pairs={{0,4},{4,0},{8,12},{12,8},{16,20},{20,16},{24,28},{28,24},{1,5},{5... | collective-permute-start | bytes 6881288 | tf_op jit(solution)/shard_map/ppermute | solution.py:401
  193.5 156.1 %collective-permute-start.15 = (bf16[2,640,896]{2,1,0:T(8,128)(2,1)}, bf16[2,640,896]{2,1,0:T(8,128)(2,1)}, u32[]{:S(2)}, u32[]{:S(2)}) collective-permute-start(bf16[2,640,896]{2,1,0:T(8,128)(2,1)} %collective-permute-done.12.refs_5_.refs_1_), channel_id=1, source_target_pairs={{0,4},{4,0},{8,12},{12,8},{16,20},{20,16},{24,28},{28,24},{1,5},{5... | collective-permute-start | bytes 6881288 | tf_op jit(solution)/shard_map/ppermute | solution.py:401
  245.7 103.8 %collective-permute-start.16 = (bf16[2,640,896]{2,1,0:T(8,128)(2,1)}, bf16[2,640,896]{2,1,0:T(8,128)(2,1)}, u32[]{:S(2)}, u32[]{:S(2)}) collective-permute-start(bf16[2,640,896]{2,1,0:T(8,128)(2,1)} %collective-permute-done.13.refs_6_.refs_2_), channel_id=1, source_target_pairs={{0,4},{4,0},{8,12},{12,8},{16,20},{20,16},{24,28},{28,24},{1,5},{5... | collective-permute-start | bytes 6881288 | tf_op jit(solution)/shard_map/ppermute | solution.py:401
  245.7 103.8 %collective-permute-start.17 = (bf16[2,640,896]{2,1,0:T(8,128)(2,1)}, bf16[2,640,896]{2,1,0:T(8,128)(2,1)}, u32[]{:S(2)}, u32[]{:S(2)}) collective-permute-start(bf16[2,640,896]{2,1,0:T(8,128)(2,1)} %collective-permute-done.8.refs_7_.refs_3_), channel_id=1, source_target_pairs={{0,4},{4,0},{8,12},{12,8},{16,20},{20,16},{24,28},{28,24},{1,5},{5... | collective-permute-start | bytes 6881288 | tf_op jit(solution)/shard_map/ppermute | solution.py:401
  253.4 49.5 %collective-permute-start.5 = (bf16[16,896]{1,0:T(8,128)(2,1)S(1)}, bf16[16,896]{1,0:T(8,128)(2,1)S(1)}, u32[]{:S(2)}, u32[]{:S(2)}) collective-permute-start(bf16[16,896]{1,0:T(8,128)(2,1)S(1)} %get-tuple-element.143), channel_id=1, source_target_pairs={{0,16},{4,20},{8,24},{12,28},{16,0},{20,4},{24,8},{28,12},{1,17},{... | collective-permute-start | bytes 86024 | tf_op jit(solution)/shard_map/ppermute | solution.py:398
  385.2 220.4 %reduce-scatter.6.cloned.1.call-start = ((), (), s32[]{:S(2)}) async-start(), calls=%async_computation.6 | async-start | bytes 6553600 | tf_op jit(solution)/shard_map/reduce_scatter | solution.py:447
  390.5 19.2 %collective-permute-start.22 = (bf16[128,896]{1,0:T(8,128)(2,1)S(1)}, bf16[128,896]{1,0:T(8,128)(2,1)S(1)}, u32[]{:S(2)}, u32[]{:S(2)}) collective-permute-start(bf16[128,896]{1,0:T(8,128)(2,1)S(1)} %get-tuple-element.57), channel_id=1, source_target_pairs={{0,16},{4,20},{8,24},{12,28},{16,0},{20,4},{24,8},{28,12},{1,17},{... | collective-permute-start | bytes 688136 | tf_op jit(solution)/shard_map/ppermute | solution.py:398
  391.3 18.4 %collective-permute-start.23 = (bf16[128,896]{1,0:T(8,128)(2,1)S(1)}, bf16[128,896]{1,0:T(8,128)(2,1)S(1)}, u32[]{:S(2)}, u32[]{:S(2)}) collective-permute-start(bf16[128,896]{1,0:T(8,128)(2,1)S(1)} %get-tuple-element.58), channel_id=1, source_target_pairs={{0,24},{4,28},{8,16},{12,20},{16,8},{20,12},{24,0},{28,4},{1,25},{... | collective-permute-start | bytes 688136 | tf_op jit(solution)/shard_map/ppermute | solution.py:398
  451.0 165.2 %reduce-scatter.4.cloned.1.call-start = ((), (), s32[]{:S(2)}) async-start(), calls=%async_computation.5 | async-start | bytes 6553600 | tf_op jit(solution)/shard_map/reduce_scatter | solution.py:447
  517.1 30.3 %collective-permute-start.18 = (bf16[128,896]{1,0:T(8,128)(2,1)}, bf16[128,896]{1,0:T(8,128)(2,1)}, u32[]{:S(2)}, u32[]{:S(2)}) collective-permute-start(bf16[128,896]{1,0:T(8,128)(2,1)} %copy-done.48), channel_id=1, source_target_pairs={{0,8},{4,12},{8,0},{12,4},{16,24},{20,28},{24,16},{28,20},{1,9},{5... | collective-permute-start | bytes 688136 | tf_op jit(solution)/shard_map/ppermute | solution.py:398
  520.1 28.3 %collective-permute-start.19 = (bf16[128,896]{1,0:T(8,128)(2,1)}, bf16[128,896]{1,0:T(8,128)(2,1)}, u32[]{:S(2)}, u32[]{:S(2)}) collective-permute-start(bf16[128,896]{1,0:T(8,128)(2,1)} %copy-done.47), channel_id=1, source_target_pairs={{0,16},{4,20},{8,24},{12,28},{16,0},{20,4},{24,8},{28,12},{1,17},{... | collective-permute-start | bytes 688136 | tf_op jit(solution)/shard_map/ppermute | solution.py:398
  520.5 23.1 %collective-permute-start.30 = (bf16[64,896]{1,0:T(8,128)(2,1)}, bf16[64,896]{1,0:T(8,128)(2,1)S(1)}, u32[]{:S(2)}, u32[]{:S(2)}) collective-permute-start(bf16[64,896]{1,0:T(8,128)(2,1)} %copy-done.51), channel_id=1, source_target_pairs={{0,8},{4,12},{8,0},{12,4},{16,24},{20,28},{24,16},{28,20},{1,9},{5... | collective-permute-start | bytes 344072 | tf_op jit(solution)/shard_map/ppermute | solution.py:398
  522.5 21.5 %collective-permute-start.31 = (bf16[64,896]{1,0:T(8,128)(2,1)}, bf16[64,896]{1,0:T(8,128)(2,1)}, u32[]{:S(2)}, u32[]{:S(2)}) collective-permute-start(bf16[64,896]{1,0:T(8,128)(2,1)} %copy-done.50), channel_id=1, source_target_pairs={{0,16},{4,20},{8,24},{12,28},{16,0},{20,4},{24,8},{28,12},{1,17},{... | collective-permute-start | bytes 344072 | tf_op jit(solution)/shard_map/ppermute | solution.py:398
  523.1 24.3 %collective-permute-start.32 = (bf16[64,896]{1,0:T(8,128)(2,1)}, bf16[64,896]{1,0:T(8,128)(2,1)}, u32[]{:S(2)}, u32[]{:S(2)}) collective-permute-start(bf16[64,896]{1,0:T(8,128)(2,1)} %copy-done.49), channel_id=1, source_target_pairs={{0,24},{4,28},{8,16},{12,20},{16,8},{20,12},{24,0},{28,4},{1,25},{... | collective-permute-start | bytes 344072 | tf_op jit(solution)/shard_map/ppermute | solution.py:398
  537.7 40.9 %all-to-all-start = ((bf16[8,16,896]{2,1,0:T(8,128)(2,1)}), bf16[8,16,896]{2,1,0:T(8,128)(2,1)S(1)}, u32[]{:S(2)}, u32[]{:S(2)}) async-start(bf16[8,16,896]{2,1,0:T(8,128)(2,1)} %bitcast.60), calls=%async_computation.3 | async-start | bytes 458752 | tf_op jit(solution)/shard_map/all_to_all | solution.py:486
  543.6 35.1 %collective-permute-start.42 = (bf16[4,640,128]{2,1,0:T(8,128)(2,1)}, bf16[4,640,128]{2,1,0:T(8,128)(2,1)}, u32[]{:S(2)}, u32[]{:S(2)}) collective-permute-start(bf16[4,640,128]{2,1,0:T(8,128)(2,1)} %fusion.2), channel_id=1, source_target_pairs={{0,4},{4,0},{8,12},{12,8},{16,20},{20,16},{24,28},{28,24},{1,5},{5... | collective-permute-start | bytes 1966088 | tf_op jit(solution)/shard_map/ppermute | solution.py:401
  547.4 27.8 %collective-permute-start.25 = (bf16[128,896]{1,0:T(8,128)(2,1)S(1)}, bf16[128,896]{1,0:T(8,128)(2,1)S(1)}, u32[]{:S(2)}, u32[]{:S(2)}) collective-permute-start(bf16[128,896]{1,0:T(8,128)(2,1)S(1)} %copy-done.42), channel_id=1, source_target_pairs={{0,16},{4,20},{8,24},{12,28},{16,0},{20,4},{24,8},{28,12},{1,17},{... | collective-permute-start | bytes 688136 | tf_op jit(solution)/shard_map/ppermute | solution.py:398
  548.4 26.9 %collective-permute-start.26 = (bf16[128,896]{1,0:T(8,128)(2,1)S(1)}, bf16[128,896]{1,0:T(8,128)(2,1)S(1)}, u32[]{:S(2)}, u32[]{:S(2)}) collective-permute-start(bf16[128,896]{1,0:T(8,128)(2,1)S(1)} %copy-done.40), channel_id=1, source_target_pairs={{0,24},{4,28},{8,16},{12,20},{16,8},{20,12},{24,0},{28,4},{1,25},{... | collective-permute-start | bytes 688136 | tf_op jit(solution)/shard_map/ppermute | solution.py:398
  605.4 25.2 %collective-permute-start.40 = (bf16[8,16,640]{2,0,1:T(8,128)(2,1)S(1)}, bf16[8,16,640]{2,0,1:T(8,128)(2,1)}, u32[]{:S(2)}, u32[]{:S(2)}) collective-permute-start(bf16[8,16,640]{2,0,1:T(8,128)(2,1)S(1)} %bitcast.173), channel_id=1, source_target_pairs={{0,16},{4,20},{8,24},{12,28},{16,0},{20,4},{24,8},{28,12},{1,17},{... | collective-permute-start | bytes 491528 | tf_op jit(solution)/shard_map/ppermute | solution.py:398
  607.1 28.5 %collective-permute-start.39 = (bf16[8,16,640]{2,0,1:T(8,128)(2,1)S(1)}, bf16[8,16,640]{2,0,1:T(8,128)(2,1)}, u32[]{:S(2)}, u32[]{:S(2)}) collective-permute-start(bf16[8,16,640]{2,0,1:T(8,128)(2,1)S(1)} %bitcast.172), channel_id=1, source_target_pairs={{0,8},{4,12},{8,0},{12,4},{16,24},{20,28},{24,16},{28,20},{1,9},{5... | collective-permute-start | bytes 491528 | tf_op jit(solution)/shard_map/ppermute | solution.py:398
  610.2 25.4 %collective-permute-start.38 = (bf16[8,32,640]{2,0,1:T(8,128)(2,1)S(1)}, bf16[8,32,640]{2,0,1:T(8,128)(2,1)S(1)}, u32[]{:S(2)}, u32[]{:S(2)}) collective-permute-start(bf16[8,32,640]{2,0,1:T(8,128)(2,1)S(1)} %bitcast.166), channel_id=1, source_target_pairs={{0,24},{4,28},{8,16},{12,20},{16,8},{20,12},{24,0},{28,4},{1,25},{... | collective-permute-start | bytes 983048 | tf_op jit(solution)/shard_map/ppermute | solution.py:398
  612.9 47.5 %collective-permute-start.37 = (bf16[8,32,640]{2,0,1:T(8,128)(2,1)S(1)}, bf16[8,32,640]{2,0,1:T(8,128)(2,1)S(1)}, u32[]{:S(2)}, u32[]{:S(2)}) collective-permute-start(bf16[8,32,640]{2,0,1:T(8,128)(2,1)S(1)} %bitcast.167), channel_id=1, source_target_pairs={{0,16},{4,20},{8,24},{12,28},{16,0},{20,4},{24,8},{28,12},{1,17},{... | collective-permute-start | bytes 983048 | tf_op jit(solution)/shard_map/ppermute | solution.py:398
  613.3 47.2 %collective-permute-start.36 = (bf16[8,32,640]{2,0,1:T(8,128)(2,1)S(1)}, bf16[8,32,640]{2,0,1:T(8,128)(2,1)S(1)}, u32[]{:S(2)}, u32[]{:S(2)}) collective-permute-start(bf16[8,32,640]{2,0,1:T(8,128)(2,1)S(1)} %bitcast.168), channel_id=1, source_target_pairs={{0,8},{4,12},{8,0},{12,4},{16,24},{20,28},{24,16},{28,20},{1,9},{5... | collective-permute-start | bytes 983048 | tf_op jit(solution)/shard_map/ppermute | solution.py:398
  630.6 30.0 %collective-permute-start.35 = (bf16[8,32,640]{2,0,1:T(8,128)(2,1)S(1)}, bf16[8,32,640]{2,0,1:T(8,128)(2,1)S(1)}, u32[]{:S(2)}, u32[]{:S(2)}) collective-permute-start(bf16[8,32,640]{2,0,1:T(8,128)(2,1)S(1)} %bitcast.171), channel_id=1, source_target_pairs={{0,24},{4,28},{8,16},{12,20},{16,8},{20,12},{24,0},{28,4},{1,25},{... | collective-permute-start | bytes 983048 | tf_op jit(solution)/shard_map/ppermute | solution.py:398
  635.6 38.7 %collective-permute-start.34 = (bf16[8,32,640]{2,0,1:T(8,128)(2,1)S(1)}, bf16[8,32,640]{2,0,1:T(8,128)(2,1)S(1)}, u32[]{:S(2)}, u32[]{:S(2)}) collective-permute-start(bf16[8,32,640]{2,0,1:T(8,128)(2,1)S(1)} %bitcast.170), channel_id=1, source_target_pairs={{0,16},{4,20},{8,24},{12,28},{16,0},{20,4},{24,8},{28,12},{1,17},{... | collective-permute-start | bytes 983048 | tf_op jit(solution)/shard_map/ppermute | solution.py:398
  635.6 38.7 %collective-permute-start.33 = (bf16[8,32,640]{2,0,1:T(8,128)(2,1)S(1)}, bf16[8,32,640]{2,0,1:T(8,128)(2,1)S(1)}, u32[]{:S(2)}, u32[]{:S(2)}) collective-permute-start(bf16[8,32,640]{2,0,1:T(8,128)(2,1)S(1)} %bitcast.169), channel_id=1, source_target_pairs={{0,8},{4,12},{8,0},{12,4},{16,24},{20,28},{24,16},{28,20},{1,9},{5... | collective-permute-start | bytes 983048 | tf_op jit(solution)/shard_map/ppermute | solution.py:398
  (89 other events, 1824.1 us)
Sparse Core Ops, SparseCore 0:
  24.7 68.3 all-gather.3
  94.9 125.3 all-gather.5
  385.3 39.1 reduce-scatter.7
  451.1 63.3 reduce-scatter.5
  517.4 62.1 reduce-scatter.3

commit v2 on v1

--- a/solution.py
+++ b/solution.py
@@ -138,18 +138,23 @@
     n = pl.program_id(0)
     z, core, col0 = s_ref[0], s_ref[1], s_ref[2]
     tiles = pl.num_programs(0)
-    half = a_ref.shape[2]
+    half = tok_ref.shape[3] // 2
     part = b_ref.shape[2]
     step = chunk // cnt
     m_all = tok_ref.shape[1] * cnt
     rows = m_all // zs
 
-    def tok(q, m, lanes):
-        return tok_ref[q, m // cnt : m // cnt + step, :, lanes].reshape(chunk, -1)
+    def tok(q, step_at, lanes):
+        at = pl.ds(step_at * step, step)
+        return tok_ref[q, at, :, lanes].reshape(chunk, -1)
+
+    def rows_at(step_at):
+        return pl.ds(pl.multiple_of(step_at * chunk, 16), chunk)
 
     @pl.when(n == 0)
     def _():
-        for m in range(0, m_all, chunk):
+        @pl.loop(0, m_all // chunk)
+        def _(m):
             p = jnp.zeros((chunk, 2 * R), jnp.float32)
             for q in range(zs):
                 for c in range(2):
@@ -158,7 +163,7 @@
                         a_ref[jnp.bitwise_xor(core, c), jnp.bitwise_xor(z, q)],
                         preferred_element_type=jnp.float32,
                     )
-            proj_ref[m : m + chunk, :] = p.astype(jnp.bfloat16)
+            proj_ref[rows_at(m), :] = p.astype(jnp.bfloat16)
 
     for k in range(zs):
         q = jnp.bitwise_xor(z, k)
@@ -173,8 +178,10 @@
         cot_s[pl.ds(pl.multiple_of(q * rows, 16), rows), :] = cot_refs[k][...]
     keep = col0 + n >= z * tiles
     bb = split_rank(bmat_ref[...])
-    for m in range(0, m_all, chunk):
-        at = slice(m, m + chunk)
+
+    @pl.loop(0, m_all // chunk)
+    def _(m):
+        at = rows_at(m)
         acc = jnp.dot(proj_ref[at, :], bb, preferred_element_type=jnp.float32)
         for q in range(zs):
             acc += jnp.dot(tok(q, m, slice(None)), wcat_s[q], preferred_element_type=jnp.float32)
@@ -186,24 +193,36 @@
         dg = cot * u * sig * (1.0 + g * (1.0 - sig))
         dg_ref[at, :] = jnp.where(keep, dg, 0.0).astype(jnp.bfloat16)
         du_ref[at, :] = jnp.where(keep, cot * act, 0.0).astype(jnp.bfloat16)
+
     for k in range(zs):
         q = jnp.bitwise_xor(z, k)
         hid_refs[k][...] = hid_s[pl.ds(pl.multiple_of(q * rows, 16), rows), :]
 
 
 def bwd_kernel(zs, ts, cnt, s_ref, dg_ref, du_ref, bmat_ref, a_ref, *refs):
-    w_refs, (out_ref, rank_ref, d_s) = refs[: 2 * zs], refs[2 * zs :]
+    w_refs, refs = refs[: 2 * zs], refs[2 * zs :]
+    outs, (rank_ref, d_s, rank_s) = refs[:4], refs[4:]
     i = pl.program_id(0)
-    z, core = s_ref[0], s_ref[1]
+    z, core, tensor = s_ref[0], s_ref[1], s_ref[3]
     wide = dg_ref.shape[1]
+
+    def rows_of(s, k):
+        m = (jnp.bitwise_xor(z, k) * ts + jnp.bitwise_xor(tensor, s)) * cnt
+        return pl.ds(pl.multiple_of(m, 16), cnt)
 
     @pl.when(i == 0)
     def _():
-        d_s[:, :wide] = dg_ref[...]
-        d_s[:, wide : 2 * wide] = du_ref[...]
-        rank = contract_lanes(d_s[:, : 2 * wide], split_rank(bmat_ref[...]))
-        rank_ref[...] = rank
-        d_s[:, 2 * wide :] = rank.astype(jnp.bfloat16)
+        for s in range(ts):
+            for k in range(zs):
+                m = (s * zs + k) * cnt
+                d_s[m : m + cnt, :wide] = dg_ref[rows_of(s, k), :]
+                d_s[m : m + cnt, wide : 2 * wide] = du_ref[rows_of(s, k), :]
+        rank_s[...] = contract_lanes(d_s[:, : 2 * wide], split_rank(bmat_ref[...]))
+        d_s[:, 2 * wide :] = rank_s[...].astype(jnp.bfloat16)
+        for s in range(ts):
+            for k in range(zs):
+                m = (s * zs + k) * cnt
+                rank_ref[rows_of(s, k), :] = rank_s[m : m + cnt, :]
 
     for k in range(zs):
         q = jnp.bitwise_xor(z, k)
@@ -216,10 +235,14 @@
         for side in range(2):
             blk = 2 * q + jnp.bitwise_xor(core, side)
             part = acc[:, side * LANE : (side + 1) * LANE]
-            for zz in range(zs):
-                for t in range(ts):
-                    m = (zz * ts + t) * cnt
-                    out_ref[t, zz, blk] = part[m : m + cnt, :]
+            for s in range(ts):
+                for j in range(zs):
+                    m = (s * zs + j) * cnt
+                    low, first = j < zs // 2, (s & 1, s >> 1)
+                    give = first[0] if low else first[1]
+                    slot = first[1] if low else first[0]
+                    out = outs[2 * (not low) + give]
+                    out[slot, j % (zs // 2), blk] = part[m : m + cnt, :]
 
 
 def place_kernel(zs, ts, own, sizes, wide, limit, s_ref, *refs):
@@ -292,6 +315,7 @@
     m_all, wide = d_gate.shape
     half = weights[0].shape[1]
     bf = jnp.bfloat16
+    quarter = (ts // 2, zs // 2, 2 * zs, cnt)
     return pl.pallas_call(
         functools.partial(bwd_kernel, zs, ts, cnt),
         grid_spec=pltpu.PrefetchScalarGridSpec(
@@ -300,16 +324,15 @@
             in_specs=[whole(d_gate.shape), whole(d_up.shape), whole(bmat.shape)]
             + [pl.BlockSpec((2, zs, LANE, 2 * R), lambda i, s: (0, 0, i, 0))]
             + [pl.BlockSpec((2, LANE, wide), lambda i, s: (0, i, 0))] * (2 * zs),
-            out_specs=[
-                pl.BlockSpec((ts, zs, 2 * zs, cnt, LANE), lambda i, s: (0, 0, 0, 0, i)),
-                pl.BlockSpec((m_all, 2 * R), lambda i, s: (0, 0)),
+            out_specs=[pl.BlockSpec((*quarter, LANE), lambda i, s: (0, 0, 0, 0, i))] * 4
+            + [pl.BlockSpec((m_all, 2 * R), lambda i, s: (0, 0))],
+            scratch_shapes=[
+                pltpu.VMEM((m_all, 2 * wide + 2 * R), bf),
+                pltpu.VMEM((m_all, 2 * R), jnp.float32),
             ],
-            scratch_shapes=[pltpu.VMEM((m_all, 2 * wide + 2 * R), bf)],
-        ),
-        out_shape=[
-            jax.ShapeDtypeStruct((ts, zs, 2 * zs, cnt, half), bf),
-            jax.ShapeDtypeStruct((m_all, 2 * R), jnp.float32),
-        ],
+        ),
+        out_shape=[jax.ShapeDtypeStruct((*quarter, half), bf)] * 4
+        + [jax.ShapeDtypeStruct((m_all, 2 * R), jnp.float32)],
         compiler_params=pltpu.CompilerParams(vmem_limit_bytes=44 << 20),
         cost_estimate=pl.CostEstimate(
             flops=2 * m_all * 2 * wide * (2 * zs * half),
@@ -318,6 +341,33 @@
         ),
         name="bwd_columns",
     )(scalars, d_gate, d_up, bmat, a_all, *weights)
+
+
+def pack(scalars, gate_weight, up_weight, k, wide, limit):
+    half = gate_weight.shape[0]
+
+    def tile(i, s):
+        return (0, jnp.minimum(jnp.bitwise_xor(s[0], k) * wide, limit) // LANE + i)
+
+    def kernel(s_ref, gate_ref, up_ref, out_ref):
+        out_ref[0] = gate_ref[...]
+        out_ref[1] = up_ref[...]
+
+    return pl.pallas_call(
+        kernel,
+        grid_spec=pltpu.PrefetchScalarGridSpec(
+            num_scalar_prefetch=1,
+            grid=(wide // LANE,),
+            in_specs=[pl.BlockSpec((half, LANE), tile)] * 2,
+            out_specs=pl.BlockSpec((2, half, LANE), lambda i, s: (0, 0, i)),
+        ),
+        out_shape=jax.ShapeDtypeStruct((2, half, wide), jnp.bfloat16),
+        compiler_params=pltpu.CompilerParams(vmem_limit_bytes=56 << 20),
+        cost_estimate=pl.CostEstimate(
+            flops=0, bytes_accessed=8 * half * wide, transcendentals=0
+        ),
+        name="pack_columns",
+    )(scalars, gate_weight, up_weight)
 
 
 def place(scalars, pieces, zs, ts, own, sizes, cols):
@@ -400,7 +450,13 @@
     def over_core(value):
         return lax.ppermute(value, "seq", [(s, s ^ 1) for s in range(seq_count)])
 
-    scalars = jnp.stack([z, core, start_of(z) // LANE]).astype(jnp.int32)
+    def over_tensor(value, k):
+        return lax.ppermute(value, "tensor", [(t, t ^ k) for t in range(ts)])
+
+    def wide_of(value):
+        return value.astype(jnp.float32)
+
+    scalars = jnp.stack([z, core, start_of(z) // LANE, tensor]).astype(jnp.int32)
 
     a_theta, scale_a = sample(a_mean, a_hess, a_noise)
     b_theta, scale_b = sample(b_mean, b_hess, b_noise)
@@ -411,52 +467,58 @@
     a_all = jnp.stack([a_mine, over_core(a_mine)])
     b_all = jnp.stack([b_mine, over_core(b_mine)])
 
-    pieces = [jnp.stack([columns(gate_weight, k), columns(up_weight, k)]) for k in range(zs)]
+    pieces = [pack(scalars, gate_weight, up_weight, k, wide, cols - wide) for k in range(zs)]
     mine = [None] * zs
     mine[0] = pieces[0]
     for k in range(zs - 1, 0, -1):
         mine[k] = over_z(pieces[k], k)
     weights = mine + [over_core(piece) for piece in mine]
 
+    sizes = chunk_sizes(own)
     quarter = d_model // ts
     tok = lax.dynamic_slice_in_dim(tokens, tensor * quarter, quarter, 1)
-    tok = after(tok, *pieces)
     tok = lax.all_gather(tok, "seq", axis=0, axis_index_groups=cores, tiled=True)
     tok = lax.all_gather(tok, "tensor", axis=0, tiled=False)
 
-    sizes = chunk_sizes(own)
-    cots, gate = [], mine[zs - 1]
-    for off, cnt in sizes:
+    def cotangent_of(j, *earlier):
+        off, cnt = sizes[j]
         cot = cotangent.reshape(ts, own, cols)[:, off : off + cnt].reshape(ts * cnt, cols)
-        cots.append(
-            [over_z(after(columns(cot, k), gate) if k else columns(cot, k), k) for k in range(zs)]
+        cot = [columns(cot, k) for k in range(zs)]
+        cot[1:] = [over_z(after(cot[k], *earlier), k) for k in range(1, zs)]
+        return cot
+
+    cot = cotangent_of(0)
+    tok = tok.reshape(zs, zs * ts, own, quarter)
+
+    hidden, grads, ranks = [], [], []
+    d_all = []
+    for j, (off, cnt) in enumerate(sizes):
+        *hid, d_gate, d_up, bmat, proj = forward(scalars, tok, a_all, b_all, cot, weights, off, cnt)
+        if j + 1 < len(sizes):
+            cot = cotangent_of(j + 1, bmat)
+        hidden += [over_z(hid[k], k) for k in range(zs)]
+        x_keep, x_give, y_keep, y_give, rank = backward(
+            scalars, d_gate, d_up, bmat, a_all, weights, ts, cnt
         )
-        gate = mine[zs - 1], mine[zs - 2]
-    tok = tok.reshape(zs, zs * ts, own, quarter)
-
-    hidden, grads, ranks = [], [], []
-    b_part = jnp.zeros((2 * R, wide), jnp.float32)
-    for (off, cnt), cot in zip(sizes, cots):
-        *hid, d_gate, d_up, bmat, proj = forward(scalars, tok, a_all, b_all, cot, weights, off, cnt)
-        hidden += [over_z(hid[k], k) for k in range(zs)]
-        term, rank = backward(scalars, d_gate, d_up, bmat, a_all, weights, ts, cnt)
         ranks.append(rank.reshape(zs * ts, cnt, 2 * R))
-        b_part = b_part + jnp.concatenate(
-            [contract_rows(proj[:, :R], d_gate), contract_rows(proj[:, R:], d_up)], axis=0
-        )
-        term = lax.psum_scatter(
-            term.reshape(-1, half), "tensor", scatter_dimension=0, tiled=True
-        ).reshape(term.shape[1:])
-        total = jnp.zeros(term.shape[1:], jnp.float32)
-        for k in range(zs):
-            piece = lax.dynamic_index_in_dim(term, jnp.bitwise_xor(z, k), 0, keepdims=False)
-            total = total + over_z(piece, k).astype(jnp.float32)
+        d_all.append((proj, d_gate, d_up))
+        x_got, y_got = over_tensor(x_give, 1), over_tensor(y_give, 2)
+        x_next = (wide_of(x_keep[1]) + wide_of(x_got[1])).astype(bf)
+        y_next = (wide_of(y_keep[1]) + wide_of(y_got[1])).astype(bf)
+        x_last, y_last = over_tensor(x_next, 2), over_tensor(y_next, 1)
+        parts = []
+        for keep, got, last in ((x_keep, x_got, x_last), (y_keep, y_got, y_last)):
+            for k in range(zs // 2):
+                parts.append(wide_of(keep[0, k]) + wide_of(got[0, k]) + wide_of(last[k]))
+        near = [over_z(parts[k].astype(bf), 1) for k in range(1, zs, 2)]
+        parts = [parts[k] + wide_of(near[k // 2]) for k in range(0, zs, 2)]
+        total = parts[0] + wide_of(over_z(parts[1].astype(bf), 2))
         grads.append(total.astype(bf))
 
     hidden = place(scalars, hidden, zs, ts, own, sizes, cols)
     grad_tokens = jnp.concatenate(grads, axis=1).transpose(1, 0, 2).reshape(own, d_model)
 
-    rank = jnp.concatenate(ranks, axis=1).reshape(zs * rows, 2 * R)
+    rank = jnp.concatenate(ranks, axis=1).reshape(-1, 2 * R)
     rank_high = rank.astype(bf)
     rank_low = (rank - rank_high.astype(jnp.float32)).astype(bf)
     both = jnp.concatenate([rank_high, rank_low], axis=1)
@@ -478,10 +540,13 @@
     a_seq = a_seq.astype(bf)
     a_grad = a_seq.astype(jnp.float32)
     for k in range(1, ts):
-        a_grad = a_grad + lax.ppermute(
-            a_seq, "tensor", [(t, t ^ k) for t in range(ts)]
-        ).astype(jnp.float32)
-
+        a_grad = a_grad + wide_of(over_tensor(a_seq, k))
+
+    b_part = jnp.zeros((2 * R, wide), jnp.float32)
+    for left, d_gate, d_up in d_all:
+        b_part = b_part + jnp.concatenate(
+            [contract_rows(left[:, :R], d_gate), contract_rows(left[:, R:], d_up)], axis=0
+        )
     b_part = (b_part / math.sqrt(tokens_all * R)).astype(bf)
     b_parts = lax.all_to_all(
         b_part.reshape(seq_count, part, wide), "seq", 0, 0, tiled=True
@@ -506,7 +571,7 @@
     wide = -(-cols // (zs * LANE)) * LANE
     fits = (
         seq_count == 2 * ts
-        and ts & (ts - 1) == 0
+        and ts == 4
         and half % LANE == 0
         and cols % LANE == 0
         and (zs - 1) * wide < cols

time: 684 us -> 706 us (1.032)
  Pallas kernels: 109 us -> 136 us
  local copies, waits for them, and re-layouts: 43 us -> 21.7 us
  waiting for transfers between devices: 341 us -> 361 us
  starting transfers between devices: 145 us -> 136 us
    ppermute x3 -> x15, waiting for transfers between devices: 0.01 us -> 71.8 us  [over_tensor(): return lax.ppermute(value, 'tensor', [(t, t ^ k) for t in range(ts)])]
    ppermute x39, waiting for transfers between devices: 272 us -> 221 us  [over_z(): lax.ppermute(value, 'seq', [(s, s ^ 2 * k) for s in range(seq_count)])]
    pallas_call x0 -> x4, Pallas kernels: none -> 25.1 us  [pack(): pl.pallas_call(kernel, grid_spec=pltpu.PrefetchScalarGridSpec(num_scalar_...]
    ppermute x39, starting transfers between devices: 135 us -> 113 us  [over_z(): lax.ppermute(value, 'seq', [(s, s ^ 2 * k) for s in range(seq_count)])]
    ppermute x3 -> x15, starting transfers between devices: 3.55 us -> 17.4 us  [over_tensor(): return lax.ppermute(value, 'tensor', [(t, t ^ k) for t in range(ts)])]
    convert_element_type x0 -> x15, other arithmetic: none -> 11.7 us  [the longest x6 4.39 us: split_plan(): near = [over_z(parts[k].astype(bf), 1) for k in range(1, zs, 2)]]
    another operation x1 -> x0, local copies, waits for them, and re-layouts: 9.4 us -> none  [split_plan(): jnp.stack([columns(gate_weight, k), columns(up_weight, k)])]
    unnamed x133 -> x112, local copies, waits for them, and re-layouts: 20.3 us -> 14.9 us
  transfers between devices with their start and end apart: 55 -> 64, of which waited for: 24 -> 24; matrix products, arithmetic and copies ran while one was open for 6% -> 6% of each run, Pallas kernels for 12% -> 16%
where the time goes in v2:
time: 706 us; the launch traced here: 705 us
  waiting for transfers between devices  361 us (51%)
  starting transfers between devices  136 us (19%)
  Pallas kernels  136 us (19%)
  other arithmetic  26.9 us (4%)
  local copies, waits for them, and re-layouts  21.7 us (3%)
  between operations  14.9 us (2%)
  matrix products  8.91 us (1%)
    ppermute x39, waiting for transfers between devices, over_z(): lax.ppermute(value, 'seq', [(s, s ^ 2 * k) for s in range(seq_count)])  221 us
    ppermute x39, starting transfers between devices, over_z(): lax.ppermute(value, 'seq', [(s, s ^ 2 * k) for s in range(seq_count)])  113 us
    ppermute x15, waiting for transfers between devices, over_tensor(): return lax.ppermute(value, 'tensor', [(t, t ^ k) for t in range(ts)])  71.8 us
    all_gather x1, waiting for transfers between devices, split_plan(): lax.all_gather(tok, 'seq', axis=0, axis_index_groups=cores, tiled=True)  68.4 us
    pallas_call x3, Pallas kernels, forward(): pl.pallas_call(functools.partial(fwd_kernel, zs, cnt, chunk), grid_spec=p...  62.7 us
    pallas_call x3, Pallas kernels, backward(): pl.pallas_call(functools.partial(bwd_kernel, zs, ts, cnt), grid_spec=pltp...  44.7 us
    pallas_call x4, Pallas kernels, pack(): pl.pallas_call(kernel, grid_spec=pltpu.PrefetchScalarGridSpec(num_scalar_...  25.1 us
    ppermute x15, starting transfers between devices, over_tensor(): return lax.ppermute(value, 'tensor', [(t, t ^ k) for t in range(ts)])  17.4 us
  transfers between devices with their start and end apart: 64, of which 24 were waited for; matrix products, arithmetic and copies ran while one was open for 6% of the time, Pallas kernels for 16%

profile of v2, /device:TPU:0, one launch (start us, length us, event | category | flops | bytes accessed | tf_op | source)
XLA Modules:
  0.0 704.8 jit_solution(16564060901857300838)
XLA Ops:
  10.1 68.4 %all-gather.4.cloned.1.call-done = bf16[1280,1280]{1,0:T(8,128)(2,1)} async-done(((bf16[320,1280]{1,0:T(8,128)(2,1)}), bf16[1280,1280]{1,0:T(8,128)(2,1)}) %all-gather.4.cloned.1.call-update) | async-done | bytes 3276816 | tf_op jit(solution)/shard_map/all_gather | solution.py:480
  79.3 6.2 pack_columns.5
  85.5 6.6 pack_columns.6
  93.4 6.2 pack_columns.7
  103.8 133.1 %collective-permute-done.6 = bf16[16,896]{1,0:T(8,128)(2,1)S(1)} collective-permute-done((bf16[16,896]{1,0:T(8,128)(2,1)S(1)}, bf16[16,896]{1,0:T(8,128)(2,1)S(1)}, u32[]{:S(2)}, u32[]{:S(2)}) %collective-permute-start.6) | collective-permute-done | bytes 28704 | tf_op jit(solution)/shard_map/ppermute | solution.py:448
  236.9 58.0 %collective-permute-start.4 = (bf16[16,896]{1,0:T(8,128)(2,1)S(1)}, bf16[16,896]{1,0:T(8,128)(2,1)S(1)}, u32[]{:S(2)}, u32[]{:S(2)}) collective-permute-start(bf16[16,896]{1,0:T(8,128)(2,1)S(1)} %get-tuple-element.134), channel_id=1, source_target_pairs={{0,8},{4,12},{8,0},{12,4},{16,24},{20,28},{24,16},{28,20},{1,9},{5... | collective-permute-start | bytes 86024 | tf_op jit(solution)/shard_map/ppermute | solution.py:448
  300.9 6.2 pack_columns.4.refs_4_.refs_0_
  307.0 6.2 collective-permute-start
  319.2 7.5 %collective-permute-done.8.refs_1_ = bf16[128,896]{1,0:T(8,128)(2,1)S(1)} collective-permute-done((bf16[128,896]{1,0:T(8,128)(2,1)S(1)}, bf16[128,896]{1,0:T(8,128)(2,1)S(1)}, u32[]{:S(2)}, u32[]{:S(2)}) %collective-permute-start.8) | collective-permute-done | bytes 229408 | tf_op jit(solution)/shard_map/ppermute | solution.py:448
  329.5 10.4 %collective-permute-done.9.refs_2_ = bf16[128,896]{1,0:T(8,128)(2,1)S(1)} collective-permute-done((bf16[128,896]{1,0:T(8,128)(2,1)S(1)}, bf16[128,896]{1,0:T(8,128)(2,1)S(1)}, u32[]{:S(2)}, u32[]{:S(2)}) %collective-permute-start.9) | collective-permute-done | bytes 229408 | tf_op jit(solution)/shard_map/ppermute | solution.py:448
  347.7 5.5 collective-permute-done.10.refs_3_
  358.1 23.7 %fwd_columns.3 = (bf16[128,896]{1,0:T(8,128)(2,1)S(1)}, bf16[128,896]{1,0:T(8,128)(2,1)}, bf16[128,896]{1,0:T(8,128)(2,1)}, bf16[128,896]{1,0:T(8,128)(2,1)}, bf...) custom-call(s32[4]{0:T(128)S(1)} %copy-done.16, ...), custom_call_target="tpu_custom_call" | custom-call | flops 9395240960 | bytes 27262976 | tf_op jit(solution)/shard_map/fwd_columns/pallas_call | solution.py:273
  389.4 16.7 %bwd_columns.3 = (bf16[2,2,8,32,640]{4,3,2,1,0:T(8,128)(2,1)S(1)}, bf16[2,2,8,32,640]{4,3,2,1,0:T(8,128)(2,1)}, bf16[2,2,8,32,640]{4,3,2,1,0:T(8,128)(2,1)S(1)},...) custom-call(s32[4]{0:T(128)S(1)} %copy-done.16, bf16[512,896]{1,0:T(8,128)(2,1)S(1)} %get-tuple-element.73.dg_ref, ...), custom_call_target="tpu_custom_call" | custom-call | flops 9395240960 | bytes 25427968 | tf_op jit(solution)/shard_map/bwd_columns/pallas_call | solution.py:319
  407.5 6.0 collective-permute-done.22.refs_2_
  413.6 23.8 %fwd_columns.4 = (bf16[128,896]{1,0:T(8,128)(2,1)S(1)}, bf16[128,896]{1,0:T(8,128)(2,1)}, bf16[128,896]{1,0:T(8,128)(2,1)}, bf16[128,896]{1,0:T(8,128)(2,1)S(1)}...) custom-call(s32[4]{0:T(128)S(1)} %copy-done.16, ...), custom_call_target="tpu_custom_call" | custom-call | flops 9395240960 | bytes 27262976 | tf_op jit(solution)/shard_map/fwd_columns/pallas_call | solution.py:273
  438.1 3.9 collective-permute-start.27
  444.8 16.4 %bwd_columns.4 = (bf16[2,2,8,32,640]{4,3,2,1,0:T(8,128)(2,1)S(1)}, bf16[2,2,8,32,640]{4,3,2,1,0:T(8,128)(2,1)S(1)}, bf16[2,2,8,32,640]{4,3,2,1,0:T(8,128)(2,1)S(...) custom-call(s32[4]{0:T(128)S(1)} %copy-done.16, bf16[512,896]{1,0:T(8,128)(2,1)S(1)} %get-tuple-element.79.dg_ref, ...), custom_call_target="tpu_custom_call" | custom-call | flops 9395240960 | bytes 25427968 | tf_op jit(solution)/shard_map/bwd_columns/pallas_call | solution.py:319
  469.4 15.2 %fwd_columns.5 = (bf16[64,896]{1,0:T(8,128)(2,1)S(1)}, bf16[64,896]{1,0:T(8,128)(2,1)S(1)}, bf16[64,896]{1,0:T(8,128)(2,1)S(1)}, bf16[64,896]{1,0:T(8,128)(2,1)S...) custom-call(s32[4]{0:T(128)S(1)} %copy-done.16, ...), custom_call_target="tpu_custom_call" | custom-call | flops 4697620480 | bytes 22806528 | tf_op jit(solution)/shard_map/fwd_columns/pallas_call | solution.py:273
  485.2 11.5 %bwd_columns.5 = (bf16[2,2,8,16,640]{4,3,2,1,0:T(8,128)(2,1)S(1)}, bf16[2,2,8,16,640]{4,3,2,1,0:T(8,128)(2,1)}, bf16[2,2,8,16,640]{4,3,2,1,0:T(8,128)(2,1)S(1)},...) custom-call(s32[4]{0:T(128)S(1)} %copy-done.16, bf16[256,896]{1,0:T(8,128)(2,1)S(1)} %get-tuple-element.85.dg_ref, ...), custom_call_target="tpu_custom_call" | custom-call | flops 4697620480 | bytes 21889024 | tf_op jit(solution)/shard_map/bwd_columns/pallas_call | solution.py:319
  498.6 4.3 all-to-all-start
  502.9 7.0 fusion.7
  509.9 3.6 collective-permute-start.26
  514.8 7.1 %collective-permute-done.30.refs_9_ = bf16[64,896]{1,0:T(8,128)(2,1)S(1)} collective-permute-done((bf16[64,896]{1,0:T(8,128)(2,1)S(1)}, bf16[64,896]{1,0:T(8,128)(2,1)S(1)}, u32[]{:S(2)}, u32[]{:S(2)}) %collective-permute-start.30) | collective-permute-done | bytes 114720 | tf_op jit(solution)/shard_map/ppermute | solution.py:448
  524.5 7.2 %collective-permute-done.31.refs_10_ = bf16[64,896]{1,0:T(8,128)(2,1)S(1)} collective-permute-done((bf16[64,896]{1,0:T(8,128)(2,1)S(1)}, bf16[64,896]{1,0:T(8,128)(2,1)S(1)}, u32[]{:S(2)}, u32[]{:S(2)}) %collective-permute-start.31) | collective-permute-done | bytes 114720 | tf_op jit(solution)/shard_map/ppermute | solution.py:448
  535.9 3.4 place_hidden.1
  546.7 28.6 %collective-permute-done.50 = bf16[2,2,8,16,640]{4,3,2,1,0:T(8,128)(2,1)} collective-permute-done((bf16[2,2,8,16,640]{4,3,2,1,0:T(8,128)(2,1)}, bf16[2,2,8,16,640]{4,3,2,1,0:T(8,128)(2,1)}, u32[]{:S(2)}, u32[]{:S(2)}) %collective-permute-start.50) | collective-permute-done | bytes 655392 | tf_op jit(solution)/shard_map/ppermute | solution.py:454
  591.1 29.7 %collective-permute-done.51 = bf16[2,8,16,640]{3,2,1,0:T(8,128)(2,1)S(1)} collective-permute-done((bf16[2,8,16,640]{3,2,1,0:T(8,128)(2,1)S(1)}, bf16[2,8,16,640]{3,2,1,0:T(8,128)(2,1)S(1)}, u32[]{:S(2)}, u32[]{:S(2)}) %collective-permute-start.51) | collective-permute-done | bytes 327712 | tf_op jit(solution)/shard_map/ppermute | solution.py:454
  627.6 3.5 collective-permute-done.58
  633.4 5.6 collective-permute-done.52
  648.3 6.7 collective-permute-done.44
  659.0 18.1 %collective-permute-done.45 = bf16[8,32,640]{2,1,0:T(8,128)(2,1)S(1)} collective-permute-done((bf16[8,32,640]{2,1,0:T(8,128)(2,1)S(1)}, bf16[8,32,640]{2,1,0:T(8,128)(2,1)S(1)}, u32[]{:S(2)}, u32[]{:S(2)}) %collective-permute-start.45) | collective-permute-done | bytes 327712 | tf_op jit(solution)/shard_map/ppermute | solution.py:448
  681.3 10.9 %collective-permute-done.39 = bf16[8,32,640]{2,1,0:T(8,128)(2,1)S(1)} collective-permute-done((bf16[8,32,640]{2,1,0:T(8,128)(2,1)S(1)}, bf16[8,32,640]{2,1,0:T(8,128)(2,1)S(1)}, u32[]{:S(2)}, u32[]{:S(2)}) %collective-permute-start.39) | collective-permute-done | bytes 327712 | tf_op jit(solution)/shard_map/ppermute | solution.py:448
  (275 shorter events, 122.6 us)
Async XLA Ops:
  7.2 71.4 %all-gather.4.cloned.1.call-start = ((), (), s32[]{:S(2)}) async-start(), calls=%async_computation.1 | async-start | bytes 4096000 | tf_op jit(solution)/shard_map/all_gather | solution.py:480
  10.1 343.9 %all-gather.6.cloned.1.call-start = ((), (), s32[]{:S(2)}) async-start(), calls=%async_computation.2 | async-start | bytes 16384000 | tf_op jit(solution)/shard_map/all_gather | solution.py:481
  85.5 230.4 %collective-permute-start.11 = (bf16[2,640,896]{2,1,0:T(8,128)(2,1)}, bf16[2,640,896]{2,1,0:T(8,128)(2,1)}, u32[]{:S(2)}, u32[]{:S(2)}) collective-permute-start(bf16[2,640,896]{2,1,0:T(8,128)(2,1)} %pack_columns.5), channel_id=1, source_target_pairs={{0,8},{4,12},{8,0},{12,4},{16,24},{20,28},{24,16},{28,20},{1,9},{5... | collective-permute-start | bytes 6881288 | tf_op jit(solution)/shard_map/ppermute | solution.py:448
  92.1 224.3 %collective-permute-start.12 = (bf16[2,640,896]{2,1,0:T(8,128)(2,1)}, bf16[2,640,896]{2,1,0:T(8,128)(2,1)}, u32[]{:S(2)}, u32[]{:S(2)}) collective-permute-start(bf16[2,640,896]{2,1,0:T(8,128)(2,1)} %pack_columns.6), channel_id=1, source_target_pairs={{0,16},{4,20},{8,24},{12,28},{16,0},{20,4},{24,8},{28,12},{1,17},{... | collective-permute-start | bytes 6881288 | tf_op jit(solution)/shard_map/ppermute | solution.py:448
  99.6 216.8 %collective-permute-start.13 = (bf16[2,640,896]{2,1,0:T(8,128)(2,1)}, bf16[2,640,896]{2,1,0:T(8,128)(2,1)}, u32[]{:S(2)}, u32[]{:S(2)}) collective-permute-start(bf16[2,640,896]{2,1,0:T(8,128)(2,1)} %pack_columns.7), channel_id=1, source_target_pairs={{0,24},{4,28},{8,16},{12,20},{16,8},{20,12},{24,0},{28,4},{1,25},{... | collective-permute-start | bytes 6881288 | tf_op jit(solution)/shard_map/ppermute | solution.py:448
  103.0 133.9 %collective-permute-start.6 = (bf16[16,896]{1,0:T(8,128)(2,1)S(1)}, bf16[16,896]{1,0:T(8,128)(2,1)S(1)}, u32[]{:S(2)}, u32[]{:S(2)}) collective-permute-start(bf16[16,896]{1,0:T(8,128)(2,1)S(1)} %get-tuple-element.132), channel_id=1, source_target_pairs={{0,24},{4,28},{8,16},{12,20},{16,8},{20,12},{24,0},{28,4},{1,25},{... | collective-permute-start | bytes 86024 | tf_op jit(solution)/shard_map/ppermute | solution.py:448
  103.8 191.1 %collective-permute-start.5 = (bf16[16,896]{1,0:T(8,128)(2,1)S(1)}, bf16[16,896]{1,0:T(8,128)(2,1)S(1)}, u32[]{:S(2)}, u32[]{:S(2)}) collective-permute-start(bf16[16,896]{1,0:T(8,128)(2,1)S(1)} %get-tuple-element.133), channel_id=1, source_target_pairs={{0,16},{4,20},{8,24},{12,28},{16,0},{20,4},{24,8},{28,12},{1,17},{... | collective-permute-start | bytes 86024 | tf_op jit(solution)/shard_map/ppermute | solution.py:448
  236.9 59.9 %collective-permute-start.4 = (bf16[16,896]{1,0:T(8,128)(2,1)S(1)}, bf16[16,896]{1,0:T(8,128)(2,1)S(1)}, u32[]{:S(2)}, u32[]{:S(2)}) collective-permute-start(bf16[16,896]{1,0:T(8,128)(2,1)S(1)} %get-tuple-element.134), channel_id=1, source_target_pairs={{0,8},{4,12},{8,0},{12,4},{16,24},{20,28},{24,16},{28,20},{1,9},{5... | collective-permute-start | bytes 86024 | tf_op jit(solution)/shard_map/ppermute | solution.py:448
  315.8 38.1 %collective-permute-start.14 = (bf16[2,640,896]{2,1,0:T(8,128)(2,1)}, bf16[2,640,896]{2,1,0:T(8,128)(2,1)}, u32[]{:S(2)}, u32[]{:S(2)}) collective-permute-start(bf16[2,640,896]{2,1,0:T(8,128)(2,1)} %pack_columns.4.refs_4_.refs_0_), channel_id=1, source_target_pairs={{0,4},{4,0},{8,12},{12,8},{16,20},{20,16},{24,28},{28,24},{1,5},{5... | collective-permute-start | bytes 6881288 | tf_op jit(solution)/shard_map/ppermute | solution.py:451
  315.8 38.1 %collective-permute-start.15 = (bf16[2,640,896]{2,1,0:T(8,128)(2,1)}, bf16[2,640,896]{2,1,0:T(8,128)(2,1)}, u32[]{:S(2)}, u32[]{:S(2)}) collective-permute-start(bf16[2,640,896]{2,1,0:T(8,128)(2,1)} %collective-permute-done.11.refs_5_.refs_1_), channel_id=1, source_target_pairs={{0,4},{4,0},{8,12},{12,8},{16,20},{20,16},{24,28},{28,24},{1,5},{5... | collective-permute-start | bytes 6881288 | tf_op jit(solution)/shard_map/ppermute | solution.py:451
  316.3 37.6 %collective-permute-start.16 = (bf16[2,640,896]{2,1,0:T(8,128)(2,1)}, bf16[2,640,896]{2,1,0:T(8,128)(2,1)}, u32[]{:S(2)}, u32[]{:S(2)}) collective-permute-start(bf16[2,640,896]{2,1,0:T(8,128)(2,1)} %collective-permute-done.12.refs_6_.refs_2_), channel_id=1, source_target_pairs={{0,4},{4,0},{8,12},{12,8},{16,20},{20,16},{24,28},{28,24},{1,5},{5... | collective-permute-start | bytes 6881288 | tf_op jit(solution)/shard_map/ppermute | solution.py:451
  316.4 37.5 %collective-permute-start.17 = (bf16[2,640,896]{2,1,0:T(8,128)(2,1)}, bf16[2,640,896]{2,1,0:T(8,128)(2,1)}, u32[]{:S(2)}, u32[]{:S(2)}) collective-permute-start(bf16[2,640,896]{2,1,0:T(8,128)(2,1)} %collective-permute-done.13.refs_7_.refs_3_), channel_id=1, source_target_pairs={{0,4},{4,0},{8,12},{12,8},{16,20},{20,16},{24,28},{28,24},{1,5},{5... | collective-permute-start | bytes 6881288 | tf_op jit(solution)/shard_map/ppermute | solution.py:451
  381.9 128.0 %collective-permute-start.18 = (bf16[128,896]{1,0:T(8,128)(2,1)}, bf16[128,896]{1,0:T(8,128)(2,1)}, u32[]{:S(2)}, u32[]{:S(2)}) collective-permute-start(bf16[128,896]{1,0:T(8,128)(2,1)} %get-tuple-element.54), channel_id=1, source_target_pairs={{0,8},{4,12},{8,0},{12,4},{16,24},{20,28},{24,16},{28,20},{1,9},{5... | collective-permute-start | bytes 688136 | tf_op jit(solution)/shard_map/ppermute | solution.py:448
  384.2 129.2 %collective-permute-start.19 = (bf16[128,896]{1,0:T(8,128)(2,1)}, bf16[128,896]{1,0:T(8,128)(2,1)}, u32[]{:S(2)}, u32[]{:S(2)}) collective-permute-start(bf16[128,896]{1,0:T(8,128)(2,1)} %get-tuple-element.55), channel_id=1, source_target_pairs={{0,16},{4,20},{8,24},{12,28},{16,0},{20,4},{24,8},{28,12},{1,17},{... | collective-permute-start | bytes 688136 | tf_op jit(solution)/shard_map/ppermute | solution.py:448
  386.5 27.0 %collective-permute-start.22 = (bf16[128,896]{1,0:T(8,128)(2,1)S(1)}, bf16[128,896]{1,0:T(8,128)(2,1)S(1)}, u32[]{:S(2)}, u32[]{:S(2)}) collective-permute-start(bf16[128,896]{1,0:T(8,128)(2,1)S(1)} %copy-done.51), channel_id=1, source_target_pairs={{0,16},{4,20},{8,24},{12,28},{16,0},{20,4},{24,8},{28,12},{1,17},{... | collective-permute-start | bytes 688136 | tf_op jit(solution)/shard_map/ppermute | solution.py:448
  464.9 49.0 %collective-permute-start.20 = (bf16[128,896]{1,0:T(8,128)(2,1)}, bf16[128,896]{1,0:T(8,128)(2,1)}, u32[]{:S(2)}, u32[]{:S(2)}) collective-permute-start(bf16[128,896]{1,0:T(8,128)(2,1)} %get-tuple-element.56), channel_id=1, source_target_pairs={{0,24},{4,28},{8,16},{12,20},{16,8},{20,12},{24,0},{28,4},{1,25},{... | collective-permute-start | bytes 688136 | tf_op jit(solution)/shard_map/ppermute | solution.py:448
  466.7 68.0 %collective-permute-start.24 = (bf16[128,896]{1,0:T(8,128)(2,1)}, bf16[128,896]{1,0:T(8,128)(2,1)}, u32[]{:S(2)}, u32[]{:S(2)}) collective-permute-start(bf16[128,896]{1,0:T(8,128)(2,1)} %get-tuple-element.62), channel_id=1, source_target_pairs={{0,8},{4,12},{8,0},{12,4},{16,24},{20,28},{24,16},{28,20},{1,9},{5... | collective-permute-start | bytes 688136 | tf_op jit(solution)/shard_map/ppermute | solution.py:448
  466.9 68.4 %collective-permute-start.25 = (bf16[128,896]{1,0:T(8,128)(2,1)}, bf16[128,896]{1,0:T(8,128)(2,1)}, u32[]{:S(2)}, u32[]{:S(2)}) collective-permute-start(bf16[128,896]{1,0:T(8,128)(2,1)} %get-tuple-element.63), channel_id=1, source_target_pairs={{0,16},{4,20},{8,24},{12,28},{16,0},{20,4},{24,8},{28,12},{1,17},{... | collective-permute-start | bytes 688136 | tf_op jit(solution)/shard_map/ppermute | solution.py:448
  498.6 40.7 %all-to-all-start = ((bf16[8,16,896]{2,1,0:T(8,128)(2,1)}), bf16[8,16,896]{2,1,0:T(8,128)(2,1)}, u32[]{:S(2)}, u32[]{:S(2)}) async-start(bf16[8,16,896]{2,1,0:T(8,128)(2,1)} %bitcast.190), calls=%async_computation | async-start | bytes 458752 | tf_op jit(solution)/shard_map/all_to_all | solution.py:551
  531.8 54.3 %collective-permute-start.36 = (bf16[2,2,8,32,640]{4,3,2,1,0:T(8,128)(2,1)}, bf16[2,2,8,32,640]{4,3,2,1,0:T(8,128)(2,1)}, u32[]{:S(2)}, u32[]{:S(2)}) collective-permute-start(bf16[2,2,8,32,640]{4,3,2,1,0:T(8,128)(2,1)} %get-tuple-element.78), channel_id=1, source_target_pairs={{0,2},{1,3},{2,0},{3,1},{4,6},{5,7},{6,4},{7,5},{8,10},{9,11},{10,... | collective-permute-start | bytes 3932168 | tf_op jit(solution)/shard_map/ppermute | solution.py:454
  533.3 55.7 %collective-permute-start.33 = (bf16[2,2,8,32,640]{4,3,2,1,0:T(8,128)(2,1)}, bf16[2,2,8,32,640]{4,3,2,1,0:T(8,128)(2,1)}, u32[]{:S(2)}, u32[]{:S(2)}) collective-permute-start(bf16[2,2,8,32,640]{4,3,2,1,0:T(8,128)(2,1)} %get-tuple-element.76), channel_id=1, source_target_pairs={{0,1},{1,0},{2,3},{3,2},{4,5},{5,4},{6,7},{7,6},{8,9},{9,8},{10,11... | collective-permute-start | bytes 3932168 | tf_op jit(solution)/shard_map/ppermute | solution.py:454
  534.8 40.6 %collective-permute-start.50 = (bf16[2,2,8,16,640]{4,3,2,1,0:T(8,128)(2,1)}, bf16[2,2,8,16,640]{4,3,2,1,0:T(8,128)(2,1)}, u32[]{:S(2)}, u32[]{:S(2)}) collective-permute-start(bf16[2,2,8,16,640]{4,3,2,1,0:T(8,128)(2,1)} %get-tuple-element.91), channel_id=1, source_target_pairs={{0,2},{1,3},{2,0},{3,1},{4,6},{5,7},{6,4},{7,5},{8,10},{9,11},{10,... | collective-permute-start | bytes 1966088 | tf_op jit(solution)/shard_map/ppermute | solution.py:454
  535.3 41.2 %collective-permute-start.47 = (bf16[2,2,8,16,640]{4,3,2,1,0:T(8,128)(2,1)}, bf16[2,2,8,16,640]{4,3,2,1,0:T(8,128)(2,1)}, u32[]{:S(2)}, u32[]{:S(2)}) collective-permute-start(bf16[2,2,8,16,640]{4,3,2,1,0:T(8,128)(2,1)} %get-tuple-element.89), channel_id=1, source_target_pairs={{0,1},{1,0},{2,3},{3,2},{4,5},{5,4},{6,7},{7,6},{8,9},{9,8},{10,11... | collective-permute-start | bytes 1966088 | tf_op jit(solution)/shard_map/ppermute | solution.py:454
  544.2 36.2 %collective-permute-start.57 = (bf16[640,128]{1,0:T(8,128)(2,1)S(1)}, bf16[640,128]{1,0:T(8,128)(2,1)S(1)}, u32[]{:S(2)}, u32[]{:S(2)}) collective-permute-start(bf16[640,128]{1,0:T(8,128)(2,1)S(1)} %get-tuple-element.117), channel_id=1, source_target_pairs={{0,24},{4,28},{8,16},{12,20},{16,8},{20,12},{24,0},{28,4},{1,25},{... | collective-permute-start | bytes 491528 | tf_op jit(solution)/shard_map/ppermute | solution.py:448
  580.4 59.7 %collective-permute-start.43 = (bf16[2,2,8,32,640]{4,3,2,1,0:T(8,128)(2,1)S(1)}, bf16[2,2,8,32,640]{4,3,2,1,0:T(8,128)(2,1)S(1)}, u32[]{:S(2)}, u32[]{:S(2)}) collective-permute-start(bf16[2,2,8,32,640]{4,3,2,1,0:T(8,128)(2,1)S(1)} %copy-done.20), channel_id=1, source_target_pairs={{0,2},{1,3},{2,0},{3,1},{4,6},{5,7},{6,4},{7,5},{8,10},{9,11},{10,... | collective-permute-start | bytes 3932168 | tf_op jit(solution)/shard_map/ppermute | solution.py:454
  583.3 59.1 %collective-permute-start.40 = (bf16[2,2,8,32,640]{4,3,2,1,0:T(8,128)(2,1)S(1)}, bf16[2,2,8,32,640]{4,3,2,1,0:T(8,128)(2,1)S(1)}, u32[]{:S(2)}, u32[]{:S(2)}) collective-permute-start(bf16[2,2,8,32,640]{4,3,2,1,0:T(8,128)(2,1)S(1)} %copy-done.18), channel_id=1, source_target_pairs={{0,1},{1,0},{2,3},{3,2},{4,5},{5,4},{6,7},{7,6},{8,9},{9,8},{10,11... | collective-permute-start | bytes 3932168 | tf_op jit(solution)/shard_map/ppermute | solution.py:454
  584.7 36.0 %collective-permute-start.51 = (bf16[2,8,16,640]{3,2,1,0:T(8,128)(2,1)S(1)}, bf16[2,8,16,640]{3,2,1,0:T(8,128)(2,1)S(1)}, u32[]{:S(2)}, u32[]{:S(2)}) collective-permute-start(bf16[2,8,16,640]{3,2,1,0:T(8,128)(2,1)S(1)} %fusion.31), channel_id=1, source_target_pairs={{0,1},{1,0},{2,3},{3,2},{4,5},{5,4},{6,7},{7,6},{8,9},{9,8},{10,11... | collective-permute-start | bytes 983048 | tf_op jit(solution)/shard_map/ppermute | solution.py:454
  586.1 46.3 %collective-permute-start.48 = (bf16[2,8,16,640]{3,2,1,0:T(8,128)(2,1)S(1)}, bf16[2,8,16,640]{3,2,1,0:T(8,128)(2,1)S(1)}, u32[]{:S(2)}, u32[]{:S(2)}) collective-permute-start(bf16[2,8,16,640]{3,2,1,0:T(8,128)(2,1)S(1)} %fusion.30), channel_id=1, source_target_pairs={{0,2},{1,3},{2,0},{3,1},{4,6},{5,7},{6,4},{7,5},{8,10},{9,11},{10,... | collective-permute-start | bytes 983048 | tf_op jit(solution)/shard_map/ppermute | solution.py:454
  588.9 35.0 %collective-permute-start.60 = (bf16[640,128]{1,0:T(8,128)(2,1)S(1)}, bf16[640,128]{1,0:T(8,128)(2,1)S(1)}, u32[]{:S(2)}, u32[]{:S(2)}) collective-permute-start(bf16[640,128]{1,0:T(8,128)(2,1)S(1)} %fusion.34), channel_id=1, source_target_pairs={{0,3},{1,2},{2,1},{3,0},{4,7},{5,6},{6,5},{7,4},{8,11},{9,10},{10,... | collective-permute-start | bytes 491528 | tf_op jit(solution)/shard_map/ppermute | solution.py:454
  639.0 38.3 %collective-permute-start.49 = (bf16[8,16,640]{2,1,0:T(8,128)(2,1)S(1)}, bf16[8,16,640]{2,1,0:T(8,128)(2,1)S(1)}, u32[]{:S(2)}, u32[]{:S(2)}) collective-permute-start(bf16[8,16,640]{2,1,0:T(8,128)(2,1)S(1)} %fusion.38), channel_id=1, source_target_pairs={{0,8},{4,12},{8,0},{12,4},{16,24},{20,28},{24,16},{28,20},{1,9},{5... | collective-permute-start | bytes 491528 | tf_op jit(solution)/shard_map/ppermute | solution.py:448
  640.2 40.1 %collective-permute-start.53 = (bf16[8,16,640]{2,1,0:T(8,128)(2,1)S(1)}, bf16[8,16,640]{2,1,0:T(8,128)(2,1)S(1)}, u32[]{:S(2)}, u32[]{:S(2)}) collective-permute-start(bf16[8,16,640]{2,1,0:T(8,128)(2,1)S(1)} %fusion.37), channel_id=1, source_target_pairs={{0,16},{4,20},{8,24},{12,28},{16,0},{20,4},{24,8},{28,12},{1,17},{... | collective-permute-start | bytes 491528 | tf_op jit(solution)/shard_map/ppermute | solution.py:448
  657.4 36.0 %collective-permute-start.42 = (bf16[8,32,640]{2,1,0:T(8,128)(2,1)S(1)}, bf16[8,32,640]{2,1,0:T(8,128)(2,1)S(1)}, u32[]{:S(2)}, u32[]{:S(2)}) collective-permute-start(bf16[8,32,640]{2,1,0:T(8,128)(2,1)S(1)} %fusion.13), channel_id=1, source_target_pairs={{0,8},{4,12},{8,0},{12,4},{16,24},{20,28},{24,16},{28,20},{1,9},{5... | collective-permute-start | bytes 983048 | tf_op jit(solution)/shard_map/ppermute | solution.py:448
  (88 other events, 1792.1 us)
Sparse Core Ops, SparseCore 0:
  10.2 68.3 all-gather.3
  80.4 125.3 all-gather.5

commit v3 on v2

--- a/solution.py
+++ b/solution.py
@@ -179,9 +179,8 @@
     keep = col0 + n >= z * tiles
     bb = split_rank(bmat_ref[...])
 
-    @pl.loop(0, m_all // chunk)
-    def _(m):
-        at = rows_at(m)
+    for m in range(m_all // chunk):
+        at = slice(m * chunk, (m + 1) * chunk)
         acc = jnp.dot(proj_ref[at, :], bb, preferred_element_type=jnp.float32)
         for q in range(zs):
             acc += jnp.dot(tok(q, m, slice(None)), wcat_s[q], preferred_element_type=jnp.float32)

time: 706 us -> 704 us (level)
  no operation moved by 1% of the time
where the time goes in v3:
time: 704 us; the launch traced here: 703 us
  waiting for transfers between devices  361 us (51%)
  starting transfers between devices  136 us (19%)
  Pallas kernels  134 us (19%)
  other arithmetic  26.9 us (4%)
  local copies, waits for them, and re-layouts  21.7 us (3%)
  between operations  14.9 us (2%)
  matrix products  8.91 us (1%)
    ppermute x39, waiting for transfers between devices, over_z(): lax.ppermute(value, 'seq', [(s, s ^ 2 * k) for s in range(seq_count)])  221 us
    ppermute x39, starting transfers between devices, over_z(): lax.ppermute(value, 'seq', [(s, s ^ 2 * k) for s in range(seq_count)])  113 us
    ppermute x15, waiting for transfers between devices, over_tensor(): return lax.ppermute(value, 'tensor', [(t, t ^ k) for t in range(ts)])  71.7 us
    all_gather x1, waiting for transfers between devices, split_plan(): lax.all_gather(tok, 'seq', axis=0, axis_index_groups=cores, tiled=True)  68.4 us
    pallas_call x3, Pallas kernels, forward(): pl.pallas_call(functools.partial(fwd_kernel, zs, cnt, chunk), grid_spec=p...  60.7 us
    pallas_call x3, Pallas kernels, backward(): pl.pallas_call(functools.partial(bwd_kernel, zs, ts, cnt), grid_spec=pltp...  44.7 us
    pallas_call x4, Pallas kernels, pack(): pl.pallas_call(kernel, grid_spec=pltpu.PrefetchScalarGridSpec(num_scalar_...  25.1 us
    ppermute x15, starting transfers between devices, over_tensor(): return lax.ppermute(value, 'tensor', [(t, t ^ k) for t in range(ts)])  17.5 us
  transfers between devices with their start and end apart: 64, of which 24 were waited for; matrix products, arithmetic and copies ran while one was open for 6% of the time, Pallas kernels for 16%

profile of v3, /device:TPU:0, one launch (start us, length us, event | category | flops | bytes accessed | tf_op | source)
XLA Modules:
  0.0 702.8 jit_solution(11918295450550360461)
XLA Ops:
  10.1 68.4 %all-gather.4.cloned.1.call-done = bf16[1280,1280]{1,0:T(8,128)(2,1)} async-done(((bf16[320,1280]{1,0:T(8,128)(2,1)}), bf16[1280,1280]{1,0:T(8,128)(2,1)}) %all-gather.4.cloned.1.call-update) | async-done | bytes 3276816 | tf_op jit(solution)/shard_map/all_gather | solution.py:479
  79.3 6.2 pack_columns.5
  85.5 6.6 pack_columns.6
  93.4 6.2 pack_columns.7
  103.8 133.1 %collective-permute-done.6 = bf16[16,896]{1,0:T(8,128)(2,1)S(1)} collective-permute-done((bf16[16,896]{1,0:T(8,128)(2,1)S(1)}, bf16[16,896]{1,0:T(8,128)(2,1)S(1)}, u32[]{:S(2)}, u32[]{:S(2)}) %collective-permute-start.6) | collective-permute-done | bytes 28704 | tf_op jit(solution)/shard_map/ppermute | solution.py:447
  236.9 58.0 %collective-permute-start.4 = (bf16[16,896]{1,0:T(8,128)(2,1)S(1)}, bf16[16,896]{1,0:T(8,128)(2,1)S(1)}, u32[]{:S(2)}, u32[]{:S(2)}) collective-permute-start(bf16[16,896]{1,0:T(8,128)(2,1)S(1)} %get-tuple-element.134), channel_id=1, source_target_pairs={{0,8},{4,12},{8,0},{12,4},{16,24},{20,28},{24,16},{28,20},{1,9},{5... | collective-permute-start | bytes 86024 | tf_op jit(solution)/shard_map/ppermute | solution.py:447
  300.9 6.2 pack_columns.4.refs_4_.refs_0_
  307.0 6.2 collective-permute-start
  319.2 7.5 %collective-permute-done.8.refs_1_ = bf16[128,896]{1,0:T(8,128)(2,1)S(1)} collective-permute-done((bf16[128,896]{1,0:T(8,128)(2,1)S(1)}, bf16[128,896]{1,0:T(8,128)(2,1)S(1)}, u32[]{:S(2)}, u32[]{:S(2)}) %collective-permute-start.8) | collective-permute-done | bytes 229408 | tf_op jit(solution)/shard_map/ppermute | solution.py:447
  329.5 10.4 %collective-permute-done.9.refs_2_ = bf16[128,896]{1,0:T(8,128)(2,1)S(1)} collective-permute-done((bf16[128,896]{1,0:T(8,128)(2,1)S(1)}, bf16[128,896]{1,0:T(8,128)(2,1)S(1)}, u32[]{:S(2)}, u32[]{:S(2)}) %collective-permute-start.9) | collective-permute-done | bytes 229408 | tf_op jit(solution)/shard_map/ppermute | solution.py:447
  347.7 5.5 collective-permute-done.10.refs_3_
  358.1 22.6 %fwd_columns.3 = (bf16[128,896]{1,0:T(8,128)(2,1)S(1)}, bf16[128,896]{1,0:T(8,128)(2,1)}, bf16[128,896]{1,0:T(8,128)(2,1)}, bf16[128,896]{1,0:T(8,128)(2,1)}, bf...) custom-call(s32[4]{0:T(128)S(1)} %copy-done.16, ...), custom_call_target="tpu_custom_call" | custom-call | flops 9395240960 | bytes 27262976 | tf_op jit(solution)/shard_map/fwd_columns/pallas_call | solution.py:272
  388.3 16.7 %bwd_columns.3 = (bf16[2,2,8,32,640]{4,3,2,1,0:T(8,128)(2,1)S(1)}, bf16[2,2,8,32,640]{4,3,2,1,0:T(8,128)(2,1)}, bf16[2,2,8,32,640]{4,3,2,1,0:T(8,128)(2,1)S(1)},...) custom-call(s32[4]{0:T(128)S(1)} %copy-done.16, bf16[512,896]{1,0:T(8,128)(2,1)S(1)} %get-tuple-element.73.dg_ref, ...), custom_call_target="tpu_custom_call" | custom-call | flops 9395240960 | bytes 25427968 | tf_op jit(solution)/shard_map/bwd_columns/pallas_call | solution.py:318
  406.5 6.0 collective-permute-done.22.refs_2_
  412.5 22.9 %fwd_columns.4 = (bf16[128,896]{1,0:T(8,128)(2,1)S(1)}, bf16[128,896]{1,0:T(8,128)(2,1)}, bf16[128,896]{1,0:T(8,128)(2,1)}, bf16[128,896]{1,0:T(8,128)(2,1)S(1)}...) custom-call(s32[4]{0:T(128)S(1)} %copy-done.16, ...), custom_call_target="tpu_custom_call" | custom-call | flops 9395240960 | bytes 27262976 | tf_op jit(solution)/shard_map/fwd_columns/pallas_call | solution.py:272
  436.1 3.9 collective-permute-start.27
  442.8 16.4 %bwd_columns.4 = (bf16[2,2,8,32,640]{4,3,2,1,0:T(8,128)(2,1)S(1)}, bf16[2,2,8,32,640]{4,3,2,1,0:T(8,128)(2,1)S(1)}, bf16[2,2,8,32,640]{4,3,2,1,0:T(8,128)(2,1)S(...) custom-call(s32[4]{0:T(128)S(1)} %copy-done.16, bf16[512,896]{1,0:T(8,128)(2,1)S(1)} %get-tuple-element.79.dg_ref, ...), custom_call_target="tpu_custom_call" | custom-call | flops 9395240960 | bytes 25427968 | tf_op jit(solution)/shard_map/bwd_columns/pallas_call | solution.py:318
  467.4 15.2 %fwd_columns.5 = (bf16[64,896]{1,0:T(8,128)(2,1)S(1)}, bf16[64,896]{1,0:T(8,128)(2,1)S(1)}, bf16[64,896]{1,0:T(8,128)(2,1)S(1)}, bf16[64,896]{1,0:T(8,128)(2,1)S...) custom-call(s32[4]{0:T(128)S(1)} %copy-done.16, ...), custom_call_target="tpu_custom_call" | custom-call | flops 4697620480 | bytes 22806528 | tf_op jit(solution)/shard_map/fwd_columns/pallas_call | solution.py:272
  483.2 11.5 %bwd_columns.5 = (bf16[2,2,8,16,640]{4,3,2,1,0:T(8,128)(2,1)S(1)}, bf16[2,2,8,16,640]{4,3,2,1,0:T(8,128)(2,1)}, bf16[2,2,8,16,640]{4,3,2,1,0:T(8,128)(2,1)S(1)},...) custom-call(s32[4]{0:T(128)S(1)} %copy-done.16, bf16[256,896]{1,0:T(8,128)(2,1)S(1)} %get-tuple-element.85.dg_ref, ...), custom_call_target="tpu_custom_call" | custom-call | flops 4697620480 | bytes 21889024 | tf_op jit(solution)/shard_map/bwd_columns/pallas_call | solution.py:318
  496.6 4.3 all-to-all-start
  500.9 7.0 fusion.7
  507.9 3.6 collective-permute-start.26
  512.8 7.1 %collective-permute-done.30.refs_9_ = bf16[64,896]{1,0:T(8,128)(2,1)S(1)} collective-permute-done((bf16[64,896]{1,0:T(8,128)(2,1)S(1)}, bf16[64,896]{1,0:T(8,128)(2,1)S(1)}, u32[]{:S(2)}, u32[]{:S(2)}) %collective-permute-start.30) | collective-permute-done | bytes 114720 | tf_op jit(solution)/shard_map/ppermute | solution.py:447
  522.5 7.2 %collective-permute-done.31.refs_10_ = bf16[64,896]{1,0:T(8,128)(2,1)S(1)} collective-permute-done((bf16[64,896]{1,0:T(8,128)(2,1)S(1)}, bf16[64,896]{1,0:T(8,128)(2,1)S(1)}, u32[]{:S(2)}, u32[]{:S(2)}) %collective-permute-start.31) | collective-permute-done | bytes 114720 | tf_op jit(solution)/shard_map/ppermute | solution.py:447
  533.9 3.4 place_hidden.1
  544.7 28.6 %collective-permute-done.50 = bf16[2,2,8,16,640]{4,3,2,1,0:T(8,128)(2,1)} collective-permute-done((bf16[2,2,8,16,640]{4,3,2,1,0:T(8,128)(2,1)}, bf16[2,2,8,16,640]{4,3,2,1,0:T(8,128)(2,1)}, u32[]{:S(2)}, u32[]{:S(2)}) %collective-permute-start.50) | collective-permute-done | bytes 655392 | tf_op jit(solution)/shard_map/ppermute | solution.py:453
  589.1 29.7 %collective-permute-done.51 = bf16[2,8,16,640]{3,2,1,0:T(8,128)(2,1)S(1)} collective-permute-done((bf16[2,8,16,640]{3,2,1,0:T(8,128)(2,1)S(1)}, bf16[2,8,16,640]{3,2,1,0:T(8,128)(2,1)S(1)}, u32[]{:S(2)}, u32[]{:S(2)}) %collective-permute-start.51) | collective-permute-done | bytes 327712 | tf_op jit(solution)/shard_map/ppermute | solution.py:453
  625.5 3.4 collective-permute-done.58
  631.4 5.6 collective-permute-done.52
  646.3 6.7 collective-permute-done.44
  657.0 18.0 %collective-permute-done.45 = bf16[8,32,640]{2,1,0:T(8,128)(2,1)S(1)} collective-permute-done((bf16[8,32,640]{2,1,0:T(8,128)(2,1)S(1)}, bf16[8,32,640]{2,1,0:T(8,128)(2,1)S(1)}, u32[]{:S(2)}, u32[]{:S(2)}) %collective-permute-start.45) | collective-permute-done | bytes 327712 | tf_op jit(solution)/shard_map/ppermute | solution.py:447
  679.2 11.0 %collective-permute-done.39 = bf16[8,32,640]{2,1,0:T(8,128)(2,1)S(1)} collective-permute-done((bf16[8,32,640]{2,1,0:T(8,128)(2,1)S(1)}, bf16[8,32,640]{2,1,0:T(8,128)(2,1)S(1)}, u32[]{:S(2)}, u32[]{:S(2)}) %collective-permute-start.39) | collective-permute-done | bytes 327712 | tf_op jit(solution)/shard_map/ppermute | solution.py:447
  (275 shorter events, 122.7 us)
Async XLA Ops:
  7.2 71.4 %all-gather.4.cloned.1.call-start = ((), (), s32[]{:S(2)}) async-start(), calls=%async_computation.1 | async-start | bytes 4096000 | tf_op jit(solution)/shard_map/all_gather | solution.py:479
  10.1 343.9 %all-gather.6.cloned.1.call-start = ((), (), s32[]{:S(2)}) async-start(), calls=%async_computation.2 | async-start | bytes 16384000 | tf_op jit(solution)/shard_map/all_gather | solution.py:480
  85.5 230.4 %collective-permute-start.11 = (bf16[2,640,896]{2,1,0:T(8,128)(2,1)}, bf16[2,640,896]{2,1,0:T(8,128)(2,1)}, u32[]{:S(2)}, u32[]{:S(2)}) collective-permute-start(bf16[2,640,896]{2,1,0:T(8,128)(2,1)} %pack_columns.5), channel_id=1, source_target_pairs={{0,8},{4,12},{8,0},{12,4},{16,24},{20,28},{24,16},{28,20},{1,9},{5... | collective-permute-start | bytes 6881288 | tf_op jit(solution)/shard_map/ppermute | solution.py:447
  92.1 224.3 %collective-permute-start.12 = (bf16[2,640,896]{2,1,0:T(8,128)(2,1)}, bf16[2,640,896]{2,1,0:T(8,128)(2,1)}, u32[]{:S(2)}, u32[]{:S(2)}) collective-permute-start(bf16[2,640,896]{2,1,0:T(8,128)(2,1)} %pack_columns.6), channel_id=1, source_target_pairs={{0,16},{4,20},{8,24},{12,28},{16,0},{20,4},{24,8},{28,12},{1,17},{... | collective-permute-start | bytes 6881288 | tf_op jit(solution)/shard_map/ppermute | solution.py:447
  99.6 216.8 %collective-permute-start.13 = (bf16[2,640,896]{2,1,0:T(8,128)(2,1)}, bf16[2,640,896]{2,1,0:T(8,128)(2,1)}, u32[]{:S(2)}, u32[]{:S(2)}) collective-permute-start(bf16[2,640,896]{2,1,0:T(8,128)(2,1)} %pack_columns.7), channel_id=1, source_target_pairs={{0,24},{4,28},{8,16},{12,20},{16,8},{20,12},{24,0},{28,4},{1,25},{... | collective-permute-start | bytes 6881288 | tf_op jit(solution)/shard_map/ppermute | solution.py:447
  103.0 133.9 %collective-permute-start.6 = (bf16[16,896]{1,0:T(8,128)(2,1)S(1)}, bf16[16,896]{1,0:T(8,128)(2,1)S(1)}, u32[]{:S(2)}, u32[]{:S(2)}) collective-permute-start(bf16[16,896]{1,0:T(8,128)(2,1)S(1)} %get-tuple-element.132), channel_id=1, source_target_pairs={{0,24},{4,28},{8,16},{12,20},{16,8},{20,12},{24,0},{28,4},{1,25},{... | collective-permute-start | bytes 86024 | tf_op jit(solution)/shard_map/ppermute | solution.py:447
  103.8 191.1 %collective-permute-start.5 = (bf16[16,896]{1,0:T(8,128)(2,1)S(1)}, bf16[16,896]{1,0:T(8,128)(2,1)S(1)}, u32[]{:S(2)}, u32[]{:S(2)}) collective-permute-start(bf16[16,896]{1,0:T(8,128)(2,1)S(1)} %get-tuple-element.133), channel_id=1, source_target_pairs={{0,16},{4,20},{8,24},{12,28},{16,0},{20,4},{24,8},{28,12},{1,17},{... | collective-permute-start | bytes 86024 | tf_op jit(solution)/shard_map/ppermute | solution.py:447
  236.9 59.9 %collective-permute-start.4 = (bf16[16,896]{1,0:T(8,128)(2,1)S(1)}, bf16[16,896]{1,0:T(8,128)(2,1)S(1)}, u32[]{:S(2)}, u32[]{:S(2)}) collective-permute-start(bf16[16,896]{1,0:T(8,128)(2,1)S(1)} %get-tuple-element.134), channel_id=1, source_target_pairs={{0,8},{4,12},{8,0},{12,4},{16,24},{20,28},{24,16},{28,20},{1,9},{5... | collective-permute-start | bytes 86024 | tf_op jit(solution)/shard_map/ppermute | solution.py:447
  315.8 38.1 %collective-permute-start.14 = (bf16[2,640,896]{2,1,0:T(8,128)(2,1)}, bf16[2,640,896]{2,1,0:T(8,128)(2,1)}, u32[]{:S(2)}, u32[]{:S(2)}) collective-permute-start(bf16[2,640,896]{2,1,0:T(8,128)(2,1)} %pack_columns.4.refs_4_.refs_0_), channel_id=1, source_target_pairs={{0,4},{4,0},{8,12},{12,8},{16,20},{20,16},{24,28},{28,24},{1,5},{5... | collective-permute-start | bytes 6881288 | tf_op jit(solution)/shard_map/ppermute | solution.py:450
  315.8 38.1 %collective-permute-start.15 = (bf16[2,640,896]{2,1,0:T(8,128)(2,1)}, bf16[2,640,896]{2,1,0:T(8,128)(2,1)}, u32[]{:S(2)}, u32[]{:S(2)}) collective-permute-start(bf16[2,640,896]{2,1,0:T(8,128)(2,1)} %collective-permute-done.11.refs_5_.refs_1_), channel_id=1, source_target_pairs={{0,4},{4,0},{8,12},{12,8},{16,20},{20,16},{24,28},{28,24},{1,5},{5... | collective-permute-start | bytes 6881288 | tf_op jit(solution)/shard_map/ppermute | solution.py:450
  316.3 37.6 %collective-permute-start.16 = (bf16[2,640,896]{2,1,0:T(8,128)(2,1)}, bf16[2,640,896]{2,1,0:T(8,128)(2,1)}, u32[]{:S(2)}, u32[]{:S(2)}) collective-permute-start(bf16[2,640,896]{2,1,0:T(8,128)(2,1)} %collective-permute-done.12.refs_6_.refs_2_), channel_id=1, source_target_pairs={{0,4},{4,0},{8,12},{12,8},{16,20},{20,16},{24,28},{28,24},{1,5},{5... | collective-permute-start | bytes 6881288 | tf_op jit(solution)/shard_map/ppermute | solution.py:450
  316.4 37.5 %collective-permute-start.17 = (bf16[2,640,896]{2,1,0:T(8,128)(2,1)}, bf16[2,640,896]{2,1,0:T(8,128)(2,1)}, u32[]{:S(2)}, u32[]{:S(2)}) collective-permute-start(bf16[2,640,896]{2,1,0:T(8,128)(2,1)} %collective-permute-done.13.refs_7_.refs_3_), channel_id=1, source_target_pairs={{0,4},{4,0},{8,12},{12,8},{16,20},{20,16},{24,28},{28,24},{1,5},{5... | collective-permute-start | bytes 6881288 | tf_op jit(solution)/shard_map/ppermute | solution.py:450
  380.8 127.1 %collective-permute-start.18 = (bf16[128,896]{1,0:T(8,128)(2,1)}, bf16[128,896]{1,0:T(8,128)(2,1)}, u32[]{:S(2)}, u32[]{:S(2)}) collective-permute-start(bf16[128,896]{1,0:T(8,128)(2,1)} %get-tuple-element.54), channel_id=1, source_target_pairs={{0,8},{4,12},{8,0},{12,4},{16,24},{20,28},{24,16},{28,20},{1,9},{5... | collective-permute-start | bytes 688136 | tf_op jit(solution)/shard_map/ppermute | solution.py:447
  383.1 128.3 %collective-permute-start.19 = (bf16[128,896]{1,0:T(8,128)(2,1)}, bf16[128,896]{1,0:T(8,128)(2,1)}, u32[]{:S(2)}, u32[]{:S(2)}) collective-permute-start(bf16[128,896]{1,0:T(8,128)(2,1)} %get-tuple-element.55), channel_id=1, source_target_pairs={{0,16},{4,20},{8,24},{12,28},{16,0},{20,4},{24,8},{28,12},{1,17},{... | collective-permute-start | bytes 688136 | tf_op jit(solution)/shard_map/ppermute | solution.py:447
  385.4 27.0 %collective-permute-start.22 = (bf16[128,896]{1,0:T(8,128)(2,1)S(1)}, bf16[128,896]{1,0:T(8,128)(2,1)S(1)}, u32[]{:S(2)}, u32[]{:S(2)}) collective-permute-start(bf16[128,896]{1,0:T(8,128)(2,1)S(1)} %copy-done.51), channel_id=1, source_target_pairs={{0,16},{4,20},{8,24},{12,28},{16,0},{20,4},{24,8},{28,12},{1,17},{... | collective-permute-start | bytes 688136 | tf_op jit(solution)/shard_map/ppermute | solution.py:447
  462.9 49.0 %collective-permute-start.20 = (bf16[128,896]{1,0:T(8,128)(2,1)}, bf16[128,896]{1,0:T(8,128)(2,1)}, u32[]{:S(2)}, u32[]{:S(2)}) collective-permute-start(bf16[128,896]{1,0:T(8,128)(2,1)} %get-tuple-element.56), channel_id=1, source_target_pairs={{0,24},{4,28},{8,16},{12,20},{16,8},{20,12},{24,0},{28,4},{1,25},{... | collective-permute-start | bytes 688136 | tf_op jit(solution)/shard_map/ppermute | solution.py:447
  464.7 68.1 %collective-permute-start.24 = (bf16[128,896]{1,0:T(8,128)(2,1)}, bf16[128,896]{1,0:T(8,128)(2,1)}, u32[]{:S(2)}, u32[]{:S(2)}) collective-permute-start(bf16[128,896]{1,0:T(8,128)(2,1)} %get-tuple-element.62), channel_id=1, source_target_pairs={{0,8},{4,12},{8,0},{12,4},{16,24},{20,28},{24,16},{28,20},{1,9},{5... | collective-permute-start | bytes 688136 | tf_op jit(solution)/shard_map/ppermute | solution.py:447
  464.9 68.4 %collective-permute-start.25 = (bf16[128,896]{1,0:T(8,128)(2,1)}, bf16[128,896]{1,0:T(8,128)(2,1)}, u32[]{:S(2)}, u32[]{:S(2)}) collective-permute-start(bf16[128,896]{1,0:T(8,128)(2,1)} %get-tuple-element.63), channel_id=1, source_target_pairs={{0,16},{4,20},{8,24},{12,28},{16,0},{20,4},{24,8},{28,12},{1,17},{... | collective-permute-start | bytes 688136 | tf_op jit(solution)/shard_map/ppermute | solution.py:447
  496.6 40.7 %all-to-all-start = ((bf16[8,16,896]{2,1,0:T(8,128)(2,1)}), bf16[8,16,896]{2,1,0:T(8,128)(2,1)}, u32[]{:S(2)}, u32[]{:S(2)}) async-start(bf16[8,16,896]{2,1,0:T(8,128)(2,1)} %bitcast.190), calls=%async_computation | async-start | bytes 458752 | tf_op jit(solution)/shard_map/all_to_all | solution.py:550
  529.8 54.3 %collective-permute-start.36 = (bf16[2,2,8,32,640]{4,3,2,1,0:T(8,128)(2,1)}, bf16[2,2,8,32,640]{4,3,2,1,0:T(8,128)(2,1)}, u32[]{:S(2)}, u32[]{:S(2)}) collective-permute-start(bf16[2,2,8,32,640]{4,3,2,1,0:T(8,128)(2,1)} %get-tuple-element.78), channel_id=1, source_target_pairs={{0,2},{1,3},{2,0},{3,1},{4,6},{5,7},{6,4},{7,5},{8,10},{9,11},{10,... | collective-permute-start | bytes 3932168 | tf_op jit(solution)/shard_map/ppermute | solution.py:453
  531.3 55.7 %collective-permute-start.33 = (bf16[2,2,8,32,640]{4,3,2,1,0:T(8,128)(2,1)}, bf16[2,2,8,32,640]{4,3,2,1,0:T(8,128)(2,1)}, u32[]{:S(2)}, u32[]{:S(2)}) collective-permute-start(bf16[2,2,8,32,640]{4,3,2,1,0:T(8,128)(2,1)} %get-tuple-element.76), channel_id=1, source_target_pairs={{0,1},{1,0},{2,3},{3,2},{4,5},{5,4},{6,7},{7,6},{8,9},{9,8},{10,11... | collective-permute-start | bytes 3932168 | tf_op jit(solution)/shard_map/ppermute | solution.py:453
  532.7 40.6 %collective-permute-start.50 = (bf16[2,2,8,16,640]{4,3,2,1,0:T(8,128)(2,1)}, bf16[2,2,8,16,640]{4,3,2,1,0:T(8,128)(2,1)}, u32[]{:S(2)}, u32[]{:S(2)}) collective-permute-start(bf16[2,2,8,16,640]{4,3,2,1,0:T(8,128)(2,1)} %get-tuple-element.91), channel_id=1, source_target_pairs={{0,2},{1,3},{2,0},{3,1},{4,6},{5,7},{6,4},{7,5},{8,10},{9,11},{10,... | collective-permute-start | bytes 1966088 | tf_op jit(solution)/shard_map/ppermute | solution.py:453
  533.3 41.2 %collective-permute-start.47 = (bf16[2,2,8,16,640]{4,3,2,1,0:T(8,128)(2,1)}, bf16[2,2,8,16,640]{4,3,2,1,0:T(8,128)(2,1)}, u32[]{:S(2)}, u32[]{:S(2)}) collective-permute-start(bf16[2,2,8,16,640]{4,3,2,1,0:T(8,128)(2,1)} %get-tuple-element.89), channel_id=1, source_target_pairs={{0,1},{1,0},{2,3},{3,2},{4,5},{5,4},{6,7},{7,6},{8,9},{9,8},{10,11... | collective-permute-start | bytes 1966088 | tf_op jit(solution)/shard_map/ppermute | solution.py:453
  542.2 36.2 %collective-permute-start.57 = (bf16[640,128]{1,0:T(8,128)(2,1)S(1)}, bf16[640,128]{1,0:T(8,128)(2,1)S(1)}, u32[]{:S(2)}, u32[]{:S(2)}) collective-permute-start(bf16[640,128]{1,0:T(8,128)(2,1)S(1)} %get-tuple-element.117), channel_id=1, source_target_pairs={{0,24},{4,28},{8,16},{12,20},{16,8},{20,12},{24,0},{28,4},{1,25},{... | collective-permute-start | bytes 491528 | tf_op jit(solution)/shard_map/ppermute | solution.py:447
  578.4 59.7 %collective-permute-start.43 = (bf16[2,2,8,32,640]{4,3,2,1,0:T(8,128)(2,1)S(1)}, bf16[2,2,8,32,640]{4,3,2,1,0:T(8,128)(2,1)S(1)}, u32[]{:S(2)}, u32[]{:S(2)}) collective-permute-start(bf16[2,2,8,32,640]{4,3,2,1,0:T(8,128)(2,1)S(1)} %copy-done.20), channel_id=1, source_target_pairs={{0,2},{1,3},{2,0},{3,1},{4,6},{5,7},{6,4},{7,5},{8,10},{9,11},{10,... | collective-permute-start | bytes 3932168 | tf_op jit(solution)/shard_map/ppermute | solution.py:453
  581.2 59.1 %collective-permute-start.40 = (bf16[2,2,8,32,640]{4,3,2,1,0:T(8,128)(2,1)S(1)}, bf16[2,2,8,32,640]{4,3,2,1,0:T(8,128)(2,1)S(1)}, u32[]{:S(2)}, u32[]{:S(2)}) collective-permute-start(bf16[2,2,8,32,640]{4,3,2,1,0:T(8,128)(2,1)S(1)} %copy-done.18), channel_id=1, source_target_pairs={{0,1},{1,0},{2,3},{3,2},{4,5},{5,4},{6,7},{7,6},{8,9},{9,8},{10,11... | collective-permute-start | bytes 3932168 | tf_op jit(solution)/shard_map/ppermute | solution.py:453
  582.7 36.0 %collective-permute-start.51 = (bf16[2,8,16,640]{3,2,1,0:T(8,128)(2,1)S(1)}, bf16[2,8,16,640]{3,2,1,0:T(8,128)(2,1)S(1)}, u32[]{:S(2)}, u32[]{:S(2)}) collective-permute-start(bf16[2,8,16,640]{3,2,1,0:T(8,128)(2,1)S(1)} %fusion.31), channel_id=1, source_target_pairs={{0,1},{1,0},{2,3},{3,2},{4,5},{5,4},{6,7},{7,6},{8,9},{9,8},{10,11... | collective-permute-start | bytes 983048 | tf_op jit(solution)/shard_map/ppermute | solution.py:453
  584.1 46.3 %collective-permute-start.48 = (bf16[2,8,16,640]{3,2,1,0:T(8,128)(2,1)S(1)}, bf16[2,8,16,640]{3,2,1,0:T(8,128)(2,1)S(1)}, u32[]{:S(2)}, u32[]{:S(2)}) collective-permute-start(bf16[2,8,16,640]{3,2,1,0:T(8,128)(2,1)S(1)} %fusion.30), channel_id=1, source_target_pairs={{0,2},{1,3},{2,0},{3,1},{4,6},{5,7},{6,4},{7,5},{8,10},{9,11},{10,... | collective-permute-start | bytes 983048 | tf_op jit(solution)/shard_map/ppermute | solution.py:453
  586.9 35.0 %collective-permute-start.60 = (bf16[640,128]{1,0:T(8,128)(2,1)S(1)}, bf16[640,128]{1,0:T(8,128)(2,1)S(1)}, u32[]{:S(2)}, u32[]{:S(2)}) collective-permute-start(bf16[640,128]{1,0:T(8,128)(2,1)S(1)} %fusion.34), channel_id=1, source_target_pairs={{0,3},{1,2},{2,1},{3,0},{4,7},{5,6},{6,5},{7,4},{8,11},{9,10},{10,... | collective-permute-start | bytes 491528 | tf_op jit(solution)/shard_map/ppermute | solution.py:453
  637.0 38.2 %collective-permute-start.49 = (bf16[8,16,640]{2,1,0:T(8,128)(2,1)S(1)}, bf16[8,16,640]{2,1,0:T(8,128)(2,1)S(1)}, u32[]{:S(2)}, u32[]{:S(2)}) collective-permute-start(bf16[8,16,640]{2,1,0:T(8,128)(2,1)S(1)} %fusion.38), channel_id=1, source_target_pairs={{0,8},{4,12},{8,0},{12,4},{16,24},{20,28},{24,16},{28,20},{1,9},{5... | collective-permute-start | bytes 491528 | tf_op jit(solution)/shard_map/ppermute | solution.py:447
  638.2 40.0 %collective-permute-start.53 = (bf16[8,16,640]{2,1,0:T(8,128)(2,1)S(1)}, bf16[8,16,640]{2,1,0:T(8,128)(2,1)S(1)}, u32[]{:S(2)}, u32[]{:S(2)}) collective-permute-start(bf16[8,16,640]{2,1,0:T(8,128)(2,1)S(1)} %fusion.37), channel_id=1, source_target_pairs={{0,16},{4,20},{8,24},{12,28},{16,0},{20,4},{24,8},{28,12},{1,17},{... | collective-permute-start | bytes 491528 | tf_op jit(solution)/shard_map/ppermute | solution.py:447
  655.4 36.0 %collective-permute-start.42 = (bf16[8,32,640]{2,1,0:T(8,128)(2,1)S(1)}, bf16[8,32,640]{2,1,0:T(8,128)(2,1)S(1)}, u32[]{:S(2)}, u32[]{:S(2)}) collective-permute-start(bf16[8,32,640]{2,1,0:T(8,128)(2,1)S(1)} %fusion.13), channel_id=1, source_target_pairs={{0,8},{4,12},{8,0},{12,4},{16,24},{20,28},{24,16},{28,20},{1,9},{5... | collective-permute-start | bytes 983048 | tf_op jit(solution)/shard_map/ppermute | solution.py:447
  (88 other events, 1786.1 us)
Sparse Core Ops, SparseCore 0:
  10.2 68.3 all-gather.3
  80.4 125.3 all-gather.5
